TPU v7x, 32 devices: a whole 2x2x4 slice. The times are simulated.
32 devices in a mesh: gx: 4 (over x, core), gy: 8 (over z, y).
Axes of the slice: x: 2, y: 2, z: 4, core: 2. Of those that a mesh axis runs over, the one named last changes fastest.
Arguments:
- samples: bfloat16 [64, 128, 32, 256], P('gx', 'gy'), may hold values from -6 to 6
- leaf_basis: bfloat16 [64, 256], replicated, may hold values from -0.375 to 0.375
- transfer: bfloat16 [5, 64, 256], replicated, may hold values from -0.5 to 0.5
- coupling: bfloat16 [5, 7, 64, 448], replicated, may hold values from -0.15625 to 0.15625
- near_tiles: bfloat16 [9, 256, 256], replicated, may hold values from -0.125 to 0.125
- codes_local: int32 [64, 128, 4, 27], P('gx', 'gy'), may hold values from 0 to 35, as said below
- counts_local: int32 [64, 128, 4], P('gx', 'gy'), may hold values from 1 to 27, as said below
- codes_upper: int32 [40, 27], replicated, may hold values from 0 to 35, as said below
- counts_upper: int32 [40], replicated, may hold values from 1 to 27, as said below
Outputs:
- response: bfloat16 [64, 128, 32, 256], P('gx', 'gy')
Inputs may be any that keep to these rules, and one draw needn't show every extreme that they name: `codes_local`: entries [i, j, l, :] with i and j multiples of 2^l hold the list of the level-l cluster whose first leaf is (i, j); other entries are not read. Its first count entries are distinct codes a * 6 + b of clusters more than one step away from the target in some direction. `counts_local`: length of the list stored at the same position. `codes_upper`: row n is the list of the n-th cluster of level 4 and coarser, levels in order from 4, row-major within a level, each level with half the rows and columns of the one before and the last with 2 rows; first count entries distinct codes of clusters more than one step away from the target in some direction. `counts_upper`: length of the list of the same row.
All inputs are finite; a program needn't handle non-finite values.
Results may differ from a plain program's by a relative error of at most 0.0095.
Values may be sent and summed in bfloat16 or wider, within the bound.
A program may use at most 384 MiB of HBM per device.

v0:
```python
import jax
import jax.numpy as jnp
from jax import lax
from jax.sharding import PartitionSpec as P


def extended(block, sides, width):
    for axis, dim in sides:
        count = lax.axis_size(axis)
        forward = [(i, i + 1) for i in range(count - 1)]
        backward = [(target, source) for source, target in forward]
        low = lax.ppermute(
            lax.slice_in_dim(block, block.shape[dim] - width, None, axis=dim), axis, forward
        )
        high = lax.ppermute(lax.slice_in_dim(block, 0, width, axis=dim), axis, backward)
        block = jnp.concatenate([low, block, high], axis=dim)
    return block


def is_near(row_step, col_step):
    return abs(row_step) <= 1 and abs(col_step) <= 1


def project(leaf_samples, leaf_basis):
    coeffs = jnp.einsum(
        "ijvs,rs->ijvr", leaf_samples, leaf_basis, preferred_element_type=jnp.float32
    )
    return coeffs.astype(jnp.bfloat16)


def lift_level(children, matrices):
    grid_rows, grid_cols, vectors, rank_size = children.shape
    grouped = children.reshape(grid_rows // 2, 2, grid_cols // 2, 2, vectors, rank_size)
    grouped = grouped.transpose(0, 2, 4, 1, 3, 5).reshape(
        grid_rows // 2, grid_cols // 2, vectors, 4 * rank_size
    )
    parent = jnp.einsum("pqvc,sc->pqvs", grouped, matrices, preferred_element_type=jnp.float32)
    return parent.astype(jnp.bfloat16)


def spread(parent, matrices):
    grid_rows, grid_cols, vectors, rank_size = parent.shape
    carried = jnp.einsum("pqvs,sc->pqvc", parent, matrices, preferred_element_type=jnp.float32)
    carried = carried.reshape(grid_rows, grid_cols, vectors, 2, 2, rank_size).transpose(
        0, 3, 1, 4, 2, 5
    )
    return carried.reshape(2 * grid_rows, 2 * grid_cols, vectors, rank_size)


def member_table(list_codes, counts):
    slot_index = jnp.arange(list_codes.shape[-1], dtype=jnp.int32)
    active = slot_index < counts[..., None]
    matches = (list_codes[..., None] == jnp.arange(36, dtype=jnp.int32)) & active[..., None]
    return jnp.any(matches, axis=-2).astype(jnp.float32)


def couple(padded, member, matrices):
    grid_rows = padded.shape[0] - 4
    grid_cols = padded.shape[1] - 4
    vectors = padded.shape[2]
    rank_size = padded.shape[3]
    member = member.reshape(grid_rows // 2, 2, grid_cols // 2, 2, 36)
    totals = [
        [
            jnp.zeros((grid_rows // 2, grid_cols // 2, vectors, rank_size), jnp.float32)
            for col_bit in range(2)
        ]
        for row_bit in range(2)
    ]
    for code_row in range(6):
        for code_col in range(6):
            parities = [
                (row_bit, col_bit)
                for row_bit in range(2)
                for col_bit in range(2)
                if not is_near(code_row - 2 - row_bit, code_col - 2 - col_bit)
            ]
            if not parities:
                continue
            source = padded[
                code_row : code_row + grid_rows : 2, code_col : code_col + grid_cols : 2
            ]
            blocks = jnp.concatenate(
                [
                    matrices[
                        code_row + 1 - row_bit,
                        :,
                        (code_col + 1 - col_bit) * rank_size : (code_col + 2 - col_bit) * rank_size,
                    ]
                    for row_bit, col_bit in parities
                ],
                axis=0,
            )
            images = jnp.einsum("pqvr,sr->pqvs", source, blocks, preferred_element_type=jnp.float32)
            for number, (row_bit, col_bit) in enumerate(parities):
                weight_mask = member[:, row_bit, :, col_bit, code_row * 6 + code_col]
                totals[row_bit][col_bit] = (
                    totals[row_bit][col_bit]
                    + weight_mask[..., None, None]
                    * images[..., number * rank_size : (number + 1) * rank_size]
                )
    stacked = jnp.stack([jnp.stack(totals[row_bit], axis=0) for row_bit in range(2)], axis=0)
    return stacked.transpose(2, 0, 3, 1, 4, 5).reshape(grid_rows, grid_cols, vectors, rank_size)


def couple_one(padded, member, matrices, row_here, col_here):
    vectors = padded.shape[2]
    rank_size = padded.shape[3]
    window = lax.dynamic_slice(
        padded, (2 * (row_here // 2), 2 * (col_here // 2), 0, 0), (6, 6, vectors, rank_size)
    )
    row_bit = row_here % 2
    col_bit = col_here % 2
    summed = jnp.zeros((vectors, rank_size), jnp.float32)
    for code_row in range(6):
        for code_col in range(6):
            coupling_block = lax.dynamic_slice(
                matrices,
                (code_row + 1 - row_bit, 0, (code_col + 1 - col_bit) * rank_size),
                (1, rank_size, rank_size),
            )[0]
            term = jnp.einsum(
                "vr,sr->vs",
                window[code_row, code_col],
                coupling_block,
                preferred_element_type=jnp.float32,
            )
            summed = summed + member[code_row * 6 + code_col] * term
    return summed


def halo_coeffs(coeffs):
    grid_rows, grid_cols, vectors, rank_size = coeffs.shape
    flattened = coeffs.reshape(grid_rows, grid_cols, vectors * rank_size)
    padded = extended(flattened, (("gx", 0), ("gy", 1)), 2)
    return padded.reshape(grid_rows + 4, grid_cols + 4, vectors, rank_size)


def shards(
    samples,
    leaf_basis,
    transfer,
    coupling,
    near_tiles,
    codes_local,
    counts_local,
    codes_upper,
    counts_upper,
):
    patch_size = samples.shape[0]
    vectors = samples.shape[2]
    rank_size = leaf_basis.shape[0]
    levels_local = transfer.shape[0] - 1
    images = []
    rim_samples = extended(samples, (("gx", 0), ("gy", 1)), 1)
    leaf_coeffs = project(samples, leaf_basis)
    coeffs = leaf_coeffs
    for level_index in range(levels_local):
        stride = 2**level_index
        member = member_table(
            codes_local[::stride, ::stride, level_index],
            counts_local[::stride, ::stride, level_index],
        )
        padded = halo_coeffs(coeffs)
        images.append(couple(padded, member, coupling[level_index]))
        coeffs = lift_level(coeffs, transfer[level_index])
    flat_block = coeffs.reshape(1, vectors * rank_size)
    everything = lax.all_gather(flat_block, ("gx", "gy"), axis=0, tiled=True)
    block_grid = everything.reshape(lax.axis_size("gx"), lax.axis_size("gy"), vectors, rank_size)
    upper_coeffs = [block_grid]
    while upper_coeffs[-1].shape[0] > 2:
        upper_coeffs.append(lift_level(upper_coeffs[-1], transfer[levels_local]))
    row_index = lax.axis_index("gx")
    col_index = lax.axis_index("gy")
    offset = 0
    upper_images = []
    for upper_step, coeffs_here in enumerate(upper_coeffs):
        grid_cols = coeffs_here.shape[1]
        row_here = row_index // 2**upper_step
        col_here = col_index // 2**upper_step
        index_here = offset + row_here * grid_cols + col_here
        list_row = lax.dynamic_slice_in_dim(codes_upper, index_here, 1, 0)
        count_row = lax.dynamic_slice_in_dim(counts_upper, index_here, 1, 0)
        member = member_table(list_row, count_row)[0]
        padded = jnp.pad(coeffs_here, ((2, 2), (2, 2), (0, 0), (0, 0)))
        upper_images.append(couple_one(padded, member, coupling[levels_local], row_here, col_here))
        offset = offset + coeffs_here.shape[0] * grid_cols
    downward = upper_images[-1]
    for upper_step in range(len(upper_coeffs) - 2, -1, -1):
        row_here = row_index // 2**upper_step
        col_here = col_index // 2**upper_step
        child_slot = row_here % 2 * 2 + col_here % 2
        carried = jnp.einsum(
            "vs,sc->vc",
            downward.astype(jnp.bfloat16),
            transfer[levels_local],
            preferred_element_type=jnp.float32,
        )
        downward = upper_images[upper_step] + lax.dynamic_slice_in_dim(
            carried, child_slot * rank_size, rank_size, 1
        )
    downward = downward[None, None]
    for level_index in range(levels_local - 1, -1, -1):
        downward = images[level_index] + spread(
            downward.astype(jnp.bfloat16), transfer[level_index]
        )
    summed = jnp.einsum(
        "ijvr,rs->ijvs",
        downward.astype(jnp.bfloat16),
        leaf_basis,
        preferred_element_type=jnp.float32,
    )
    for step_row in range(3):
        for step_col in range(3):
            neighbour = rim_samples[
                step_row : step_row + patch_size, step_col : step_col + patch_size
            ]
            summed = summed + jnp.einsum(
                "ijvs,ts->ijvt",
                neighbour,
                near_tiles[step_row * 3 + step_col],
                preferred_element_type=jnp.float32,
            )
    return summed.astype(jnp.bfloat16)


def solution(mesh):
    placed = (
        P("gx", "gy", None, None),
        P(),
        P(),
        P(),
        P(),
        P("gx", "gy", None, None),
        P("gx", "gy", None),
        P(),
        P(),
    )
    return jax.shard_map(
        shards, mesh=mesh, in_specs=placed, out_specs=P("gx", "gy", None, None), check_vma=False
    )
```

profile of v0, /device:TPU:6, one launch (start us, length us, event | category | flops | bytes accessed | tf_op | source)
XLA Modules:
  0.0 595.6 jit_solution(12649062002211609220)
XLA Ops:
  0.8 3.4 convolution_convert_fusion
  4.2 3.5 copy.86
  7.7 5.3 reshape.1396
  20.4 3.0 collective-permute-start.12
  27.2 3.8 collective-permute-start.17
  32.7 2.4 collective-permute-start
  63.3 2.7 fusion.11
  66.1 2.8 slice_reduce_fusion.102
  68.8 3.7 slice_reduce_fusion.103
  72.5 3.7 slice_reduce_fusion.104
  76.3 3.7 slice_reduce_fusion.105
  79.9 3.7 slice_reduce_fusion.106
  83.6 3.9 slice_reduce_fusion.107
  89.9 66.2 %all-gather = bf16[32,1,2048]{2,1,0:T(2,128)(2,1)S(1)} all-gather(bf16[1,1,2048]{2,1,0:T(2,128)(2,1)S(1)} %reshape.1450), channel_id=1, replica_groups=mesh['gx'=4,'gy'=8] {'gx','gy'}, dimensions={0}, use_global_device_ids=true | all-gather | bytes 135168 | tf_op jit(solution)/shard_map/all_gather | solution.py:168
  158.0 2.7 fusion.1844
  188.4 6.7 %fusion.388 = f32[16,16,32,256]{3,2,1,0:T(8,128)} fusion(bf16[16,16,32,256]{3,2,1,0:T(8,128)(2,1)} %param.9, bf16[9,256,256]{2,1,0:T(8,128)(2,1)} %param.13), kind=kOutput, calls=%fused_computation.810 | convolution fusion | flops 1073741824 | bytes 12713984 | tf_op jit(solution)/shard_map/ijvs,ts->ijvt/dot_general | solution.py:218
  257.0 2.9 reshape.1393
  272.4 2.6 collective-permute-done.8
  278.4 3.6 collective-permute-start.5
  282.3 6.9 %collective-permute-start.15 = (bf16[6,2,2048]{2,1,0:T(2,128)(2,1)S(1)}, bf16[6,2,2048]{2,1,0:T(2,128)(2,1)S(1)}, u32[]{:S(2)}, u32[]{:S(2)}) collective-permute-start(bf16[6,2,2048]{2,1,0:T(2,128)(2,1)S(1)} %constant_dynamic-update-slice_fusion.9), channel_id=1, source_target_pairs={{1,0},{2,1},{3,2},{4,3},{5,4},{6,5},{7,6},{9,8},{10,9},{11,10},{12... | collective-permute-start | bytes 147464 | tf_op jit(solution)/shard_map/ppermute | solution.py:15
  295.3 3.6 collective-permute-start.11
  304.6 17.1 %fusion.1453 = f32[1,1,1,32,64]{4,3,0,2,1:T(8,128)S(1)} fusion(f32[1,1,32,256]{3,2,1,0:T(8,128)S(1)} %convolution_bitcast_fusion.4, f32[1,1,32,256]{3,2,1,0:T(8,128)S(1)} %convolution_bitcast_fusion.5, f32[1,1,32,256]{3,2,1,0:T(8,128)S(1)} %convolution_bitcast_fusion.6, f32[1,1,32,256]{3,2,1,0:T(8,128)S(1)} %convolution_bitcast_fusion.7, ...), kind=kLoop, calls=%fused_computation.2244 | loop fusion | flops 108544 | bytes 229484 | tf_op jit(solution)/shard_map/stack | solution.py:102
  321.7 16.7 %fusion.1480 = f32[1,1,1,32,64]{4,3,0,2,1:T(8,128)S(1)} fusion(f32[1,1,32,256]{3,2,1,0:T(8,128)S(1)} %convolution_bitcast_fusion.4, f32[1,1,32,256]{3,2,1,0:T(8,128)S(1)} %convolution_bitcast_fusion.5, f32[1,1,32,256]{3,2,1,0:T(8,128)S(1)} %convolution_bitcast_fusion.6, f32[1,1,32,256]{3,2,1,0:T(8,128)S(1)} %convolution_bitcast_fusion.7, ...), kind=kLoop, calls=%fused_computation.2298 | loop fusion | flops 108544 | bytes 229484 | tf_op jit(solution)/shard_map/stack | solution.py:102
  338.4 17.1 %fusion.1399 = f32[1,1,1,32,64]{4,3,2,1,0:T(8,128)S(1)} fusion(f32[1,1,32,256]{3,2,1,0:T(8,128)S(1)} %convolution_bitcast_fusion.4, f32[1,1,32,256]{3,2,1,0:T(8,128)S(1)} %convolution_bitcast_fusion.5, f32[1,1,32,256]{3,2,1,0:T(8,128)S(1)} %convolution_bitcast_fusion.6, f32[1,1,32,256]{3,2,1,0:T(8,128)S(1)} %convolution_bitcast_fusion.7, ...), kind=kLoop, calls=%fused_computation.2136 | loop fusion | flops 108544 | bytes 229484 | tf_op jit(solution)/shard_map/stack | solution.py:102
  355.6 16.8 %fusion.1426 = f32[1,1,1,32,64]{4,3,2,1,0:T(8,128)S(1)} fusion(f32[1,1,32,256]{3,2,1,0:T(8,128)S(1)} %convolution_bitcast_fusion.4, f32[1,1,32,256]{3,2,1,0:T(8,128)S(1)} %convolution_bitcast_fusion.5, f32[1,1,32,256]{3,2,1,0:T(8,128)S(1)} %convolution_bitcast_fusion.6, f32[1,1,32,256]{3,2,1,0:T(8,128)S(1)} %convolution_bitcast_fusion.7, ...), kind=kLoop, calls=%fused_computation.2190 | loop fusion | flops 108544 | bytes 229484 | tf_op jit(solution)/shard_map/stack | solution.py:102
  374.4 3.3 collective-permute-start.6
  391.3 3.3 collective-permute-start.7
  396.7 3.4 collective-permute-start.2
  400.1 3.2 collective-permute-start.3
  419.6 3.2 fusion.275
  425.6 3.3 fusion.329
  437.7 4.8 collective-permute-start.18
  442.5 5.5 fusion.4
  448.0 5.5 fusion
  453.5 3.2 pad_maximum_fusion.2
  456.7 5.4 reshape.1394
  494.6 12.0 %fusion.101 = f32[1,8,8,32,64]{4,3,2,1,0:T(8,128)} fusion(f32[8,8,32,256]{3,2,1,0:T(8,128)S(1)} %fusion.220, f32[8,8,32,256]{3,2,1,0:T(8,128)S(1)} %fusion.222, f32[8,8,32,256]{3,2,1,0:T(8,128)S(1)} %fusion.224, f32[8,8,32,256]{3,2,1,0:T(8,128)S(1)} %fusion.226, f32[8,8,32,256]{3,2,1,0:T(8,128)S(1)} %fusion.228, f32[8,8,32,256]{3,2,1,0:T(8,128)S(1)} %fusion.230, ...), kind=kLoop, calls=%fused_computation.295 | loop fusion | flops 6946816 | bytes 14686976 | tf_op jit(solution)/shard_map/stack | solution.py:102
  507.0 7.7 %fusion.128 = f32[1,8,8,32,64]{4,3,2,1,0:T(8,128)} fusion(f32[8,8,32,256]{3,2,1,0:T(8,128)S(1)} %fusion.220, f32[8,8,32,256]{3,2,1,0:T(8,128)S(1)} %fusion.222, f32[8,8,32,256]{3,2,1,0:T(8,128)S(1)} %fusion.224, f32[8,8,32,256]{3,2,1,0:T(8,128)S(1)} %fusion.226, f32[8,8,32,256]{3,2,1,0:T(8,128)S(1)} %fusion.228, f32[8,8,32,256]{3,2,1,0:T(8,128)S(1)} %fusion.230, ...), kind=kLoop, calls=%fused_computation.349 | loop fusion | flops 6946816 | bytes 14686976 | tf_op jit(solution)/shard_map/stack | solution.py:102
  515.1 11.6 %fusion.155 = f32[1,8,8,32,64]{4,3,2,1,0:T(8,128)} fusion(f32[8,8,32,256]{3,2,1,0:T(8,128)S(1)} %fusion.220, f32[8,8,32,256]{3,2,1,0:T(8,128)S(1)} %fusion.222, f32[8,8,32,256]{3,2,1,0:T(8,128)S(1)} %fusion.224, f32[8,8,32,256]{3,2,1,0:T(8,128)S(1)} %fusion.226, f32[8,8,32,256]{3,2,1,0:T(8,128)S(1)} %fusion.228, f32[8,8,32,256]{3,2,1,0:T(8,128)S(1)} %fusion.230, ...), kind=kLoop, calls=%fused_computation.403 | loop fusion | flops 6946816 | bytes 14686976 | tf_op jit(solution)/shard_map/stack | solution.py:102
  526.9 6.2 %fusion.182 = f32[1,8,8,32,64]{4,3,2,1,0:T(8,128)} fusion(f32[8,8,32,256]{3,2,1,0:T(8,128)S(1)} %fusion.220, f32[8,8,32,256]{3,2,1,0:T(8,128)S(1)} %fusion.222, f32[8,8,32,256]{3,2,1,0:T(8,128)S(1)} %fusion.224, f32[8,8,32,256]{3,2,1,0:T(8,128)S(1)} %fusion.226, f32[8,8,32,256]{3,2,1,0:T(8,128)S(1)} %fusion.228, f32[8,8,32,256]{3,2,1,0:T(8,128)S(1)} %fusion.230, ...), kind=kLoop, calls=%fused_computation.457 | loop fusion | flops 6946816 | bytes 14686976 | tf_op jit(solution)/shard_map/stack | solution.py:102
  533.1 2.9 maximum_bitcast_fusion.1
  537.5 4.4 fusion.1200
  541.9 5.4 fusion.16
  547.4 5.4 fusion.15
  552.8 5.4 fusion.17
  558.2 5.4 fusion.13
  563.7 5.4 fusion.14
  569.1 26.4 %add_convert_fusion = bf16[16,16,32,256]{3,2,1,0:T(8,128)(2,1)} fusion(f32[16,16,32,256]{3,2,1,0:T(8,128)} %fusion.4, f32[16,16,32,256]{3,2,1,0:T(8,128)} %fusion.15, f32[16,16,32,256]{3,2,1,0:T(8,128)} %fusion.13, f32[16,16,32,256]{3,2,1,0:T(8,128)} %fusion.388, f32[16,16,32,256]{3,2,1,0:T(8,128)} %fusion.16, f32[16,16,32,256]{3,2,1,0:T(8,128)} %fusion.14, ...), kind=kOutput, calls=%fused_computation | convolution fusion | flops 1104740352 | bytes 84836352 | tf_op jit(solution)/shard_map/ijvs,ts->ijvt/dot_general | solution.py:218
  (1133 shorter events, 238.0 us)
Async XLA Ops:
  17.3 71.6 %copy-start.6 = (bf16[4,4,32,64]{3,2,1,0:T(8,128)(2,1)}, bf16[4,4,32,64]{3,2,1,0:T(8,128)(2,1)S(1)}, u32[]{:S(2)}) copy-start(bf16[4,4,32,64]{3,2,1,0:T(8,128)(2,1)S(1)} %convolution_convert_fusion.2) | copy-start | bytes 196612
  18.5 251.2 %collective-permute-start.13 = (bf16[2,2,2048]{2,1,0:T(2,128)(2,1)}, bf16[2,2,2048]{2,1,0:T(2,128)(2,1)}, u32[]{:S(2)}, u32[]{:S(2)}) collective-permute-start(bf16[2,2,2048]{2,1,0:T(2,128)(2,1)} %reshape.1405), channel_id=1, source_target_pairs={{8,0},{16,8},{24,16},{9,1},{17,9},{25,17},{10,2},{18,10},{26,18},{... | collective-permute-start | bytes 49160 | tf_op jit(solution)/shard_map/ppermute | solution.py:15
  20.4 245.9 %collective-permute-start.12 = (bf16[2,2,2048]{2,1,0:T(2,128)(2,1)}, bf16[2,2,2048]{2,1,0:T(2,128)(2,1)}, u32[]{:S(2)}, u32[]{:S(2)}) collective-permute-start(bf16[2,2,2048]{2,1,0:T(2,128)(2,1)} %reshape.1405), channel_id=1, source_target_pairs={{0,8},{8,16},{16,24},{1,9},{9,17},{17,25},{2,10},{10,18},{18,26},{... | collective-permute-start | bytes 49160 | tf_op jit(solution)/shard_map/ppermute | solution.py:12
  25.3 406.9 %collective-permute-start.16 = (bf16[1,16,32,256]{3,2,1,0:T(8,128)(2,1)}, bf16[1,16,32,256]{3,2,1,0:T(8,128)(2,1)}, u32[]{:S(2)}, u32[]{:S(2)}) collective-permute-start(bf16[1,16,32,256]{3,2,1,0:T(8,128)(2,1)} %get-tuple-element.333), channel_id=1, source_target_pairs={{0,8},{8,16},{16,24},{1,9},{9,17},{17,25},{2,10},{10,18},{18,26},{... | collective-permute-start | bytes 786440 | tf_op jit(solution)/shard_map/ppermute | solution.py:12
  27.2 35.9 %slice-start.3 = ((s32[16,16,4]{1,2,0:T(4,128)}), s32[16,16,1]{1,2,0:T(1,128)S(1)}, s32[]{:S(2)}) async-start(s32[16,16,4]{1,2,0:T(4,128)} %param.15), calls=%async_computation.3 | async-start | bytes 16384 | tf_op jit(solution)/shard_map/slice | solution.py:162
  27.2 35.9 %slice-start.2 = ((s32[16,16,4,27]{3,2,1,0:T(4,128)}), s32[16,16,1,27]{3,2,1,0:T(1,128)S(1)}, s32[]{:S(2)}) async-start(s32[16,16,4,27]{3,2,1,0:T(4,128)} %param.14), calls=%async_computation.2 | async-start | bytes 262144 | tf_op jit(solution)/shard_map/slice | solution.py:161
  27.2 406.6 %collective-permute-start.17 = (bf16[1,16,32,256]{3,2,1,0:T(8,128)(2,1)}, bf16[1,16,32,256]{3,2,1,0:T(8,128)(2,1)}, u32[]{:S(2)}, u32[]{:S(2)}) collective-permute-start(bf16[1,16,32,256]{3,2,1,0:T(8,128)(2,1)} %get-tuple-element.334), channel_id=1, source_target_pairs={{8,0},{16,8},{24,16},{9,1},{17,9},{25,17},{10,2},{18,10},{26,18},{... | collective-permute-start | bytes 786440 | tf_op jit(solution)/shard_map/ppermute | solution.py:15
  32.7 358.6 %collective-permute-start = (bf16[2,16,2048]{2,1,0:T(8,128)(2,1)}, bf16[2,16,2048]{2,1,0:T(8,128)(2,1)}, u32[]{:S(2)}, u32[]{:S(2)}) collective-permute-start(bf16[2,16,2048]{2,1,0:T(8,128)(2,1)} %slice.4453), channel_id=1, source_target_pairs={{0,8},{8,16},{16,24},{1,9},{9,17},{17,25},{2,10},{10,18},{18,26},{... | collective-permute-start | bytes 393224 | tf_op jit(solution)/shard_map/ppermute | solution.py:12
  260.4 39.0 %copy-start.128 = (bf16[64,64]{1,0:T(8,128)(2,1)S(1)}, bf16[64,64]{1,0:T(8,128)(2,1)}, u32[]{:S(2)}) copy-start(bf16[64,64]{1,0:T(8,128)(2,1)} %get-tuple-element.477) | copy-start | bytes 24580
  260.4 39.0 %copy-start.149 = (bf16[64,64]{1,0:T(8,128)(2,1)S(1)}, bf16[64,64]{1,0:T(8,128)(2,1)}, u32[]{:S(2)}) copy-start(bf16[64,64]{1,0:T(8,128)(2,1)} %get-tuple-element.478) | copy-start | bytes 24580
  260.6 39.0 %copy-start.147 = (bf16[64,64]{1,0:T(8,128)(2,1)S(1)}, bf16[64,64]{1,0:T(8,128)(2,1)}, u32[]{:S(2)}) copy-start(bf16[64,64]{1,0:T(8,128)(2,1)} %get-tuple-element.476) | copy-start | bytes 24580
  260.6 39.1 %copy-start.248 = (bf16[64,64]{1,0:T(8,128)(2,1)S(1)}, bf16[64,64]{1,0:T(8,128)(2,1)}, u32[]{:S(2)}) copy-start(bf16[64,64]{1,0:T(8,128)(2,1)} %get-tuple-element.469) | copy-start | bytes 24580
  260.6 39.1 %copy-start.255 = (bf16[64,64]{1,0:T(8,128)(2,1)S(1)}, bf16[64,64]{1,0:T(8,128)(2,1)}, u32[]{:S(2)}) copy-start(bf16[64,64]{1,0:T(8,128)(2,1)} %get-tuple-element.470) | copy-start | bytes 24580
  263.0 36.9 %copy-start.254 = (bf16[64,64]{1,0:T(8,128)(2,1)S(1)}, bf16[64,64]{1,0:T(8,128)(2,1)}, u32[]{:S(2)}) copy-start(bf16[64,64]{1,0:T(8,128)(2,1)} %get-tuple-element.471) | copy-start | bytes 24580
  265.6 34.7 %copy-start.252 = (bf16[64,64]{1,0:T(8,128)(2,1)S(1)}, bf16[64,64]{1,0:T(8,128)(2,1)}, u32[]{:S(2)}) copy-start(bf16[64,64]{1,0:T(8,128)(2,1)} %get-tuple-element.472) | copy-start | bytes 24580
  266.3 15.9 %collective-permute-start.4 = (bf16[2,8,2048]{2,1,0:T(8,128)(2,1)S(1)}, bf16[2,8,2048]{2,1,0:T(8,128)(2,1)S(1)}, u32[]{:S(2)}, u32[]{:S(2)}) collective-permute-start(bf16[2,8,2048]{2,1,0:T(8,128)(2,1)S(1)} %slice.4751), channel_id=1, source_target_pairs={{0,8},{8,16},{16,24},{1,9},{9,17},{17,25},{2,10},{10,18},{18,26},{... | collective-permute-start | bytes 196616 | tf_op jit(solution)/shard_map/ppermute | solution.py:12
  269.7 5.2 collective-permute-start.8
  274.9 3.5 collective-permute-start.9
  278.4 10.8 %collective-permute-start.5 = (bf16[2,8,2048]{2,1,0:T(8,128)(2,1)S(1)}, bf16[2,8,2048]{2,1,0:T(8,128)(2,1)S(1)}, u32[]{:S(2)}, u32[]{:S(2)}) collective-permute-start(bf16[2,8,2048]{2,1,0:T(8,128)(2,1)S(1)} %slice.4753), channel_id=1, source_target_pairs={{8,0},{16,8},{24,16},{9,1},{17,9},{25,17},{10,2},{18,10},{26,18},{... | collective-permute-start | bytes 196616 | tf_op jit(solution)/shard_map/ppermute | solution.py:15
  282.3 10.6 %collective-permute-start.15 = (bf16[6,2,2048]{2,1,0:T(2,128)(2,1)S(1)}, bf16[6,2,2048]{2,1,0:T(2,128)(2,1)S(1)}, u32[]{:S(2)}, u32[]{:S(2)}) collective-permute-start(bf16[6,2,2048]{2,1,0:T(2,128)(2,1)S(1)} %constant_dynamic-update-slice_fusion.9), channel_id=1, source_target_pairs={{1,0},{2,1},{3,2},{4,3},{5,4},{6,5},{7,6},{9,8},{10,9},{11,10},{12... | collective-permute-start | bytes 147464 | tf_op jit(solution)/shard_map/ppermute | solution.py:15
  289.3 6.0 %collective-permute-start.14 = (bf16[6,2,2048]{2,1,0:T(2,128)(2,1)S(1)}, bf16[6,2,2048]{2,1,0:T(2,128)(2,1)S(1)}, u32[]{:S(2)}, u32[]{:S(2)}) collective-permute-start(bf16[6,2,2048]{2,1,0:T(2,128)(2,1)S(1)} %constant_dynamic-update-slice_fusion.9), channel_id=1, source_target_pairs={{0,1},{1,2},{2,3},{3,4},{4,5},{5,6},{6,7},{8,9},{9,10},{10,11},{11... | collective-permute-start | bytes 147464 | tf_op jit(solution)/shard_map/ppermute | solution.py:12
  292.9 79.6 %collective-permute-start.10 = (bf16[8,2,2048]{2,1,0:T(2,128)(2,1)S(1)}, bf16[8,2,2048]{2,1,0:T(2,128)(2,1)S(1)}, u32[]{:S(2)}, u32[]{:S(2)}) collective-permute-start(bf16[8,2,2048]{2,1,0:T(2,128)(2,1)S(1)} %get-tuple-element.512), channel_id=1, source_target_pairs={{0,1},{1,2},{2,3},{3,4},{4,5},{5,6},{6,7},{8,9},{9,10},{10,11},{11... | collective-permute-start | bytes 196616 | tf_op jit(solution)/shard_map/ppermute | solution.py:12
  295.3 79.1 %collective-permute-start.11 = (bf16[8,2,2048]{2,1,0:T(2,128)(2,1)S(1)}, bf16[8,2,2048]{2,1,0:T(2,128)(2,1)S(1)}, u32[]{:S(2)}, u32[]{:S(2)}) collective-permute-start(bf16[8,2,2048]{2,1,0:T(2,128)(2,1)S(1)} %get-tuple-element.513), channel_id=1, source_target_pairs={{1,0},{2,1},{3,2},{4,3},{5,4},{6,5},{7,6},{9,8},{10,9},{11,10},{12... | collective-permute-start | bytes 196616 | tf_op jit(solution)/shard_map/ppermute | solution.py:15
  304.2 74.3 %copy-start.39 = (bf16[64,64]{0,1:T(8,128)(2,1)S(1)}, bf16[64,64]{0,1:T(8,128)(2,1)}, u32[]{:S(2)}) copy-start(bf16[64,64]{0,1:T(8,128)(2,1)} %get-tuple-element.405) | copy-start | bytes 24580
  304.2 74.3 %copy-start.42 = (bf16[64,64]{0,1:T(8,128)(2,1)S(1)}, bf16[64,64]{0,1:T(8,128)(2,1)}, u32[]{:S(2)}) copy-start(bf16[64,64]{0,1:T(8,128)(2,1)} %get-tuple-element.400) | copy-start | bytes 24580
  304.3 74.4 %copy-start.38 = (bf16[64,64]{0,1:T(8,128)(2,1)S(1)}, bf16[64,64]{0,1:T(8,128)(2,1)}, u32[]{:S(2)}) copy-start(bf16[64,64]{0,1:T(8,128)(2,1)} %get-tuple-element.409) | copy-start | bytes 24580
  304.4 74.6 %copy-start.41 = (bf16[64,64]{0,1:T(8,128)(2,1)S(1)}, bf16[64,64]{0,1:T(8,128)(2,1)}, u32[]{:S(2)}) copy-start(bf16[64,64]{0,1:T(8,128)(2,1)} %get-tuple-element.407) | copy-start | bytes 24580
  304.4 74.5 %copy-start.43 = (bf16[64,64]{0,1:T(8,128)(2,1)S(1)}, bf16[64,64]{0,1:T(8,128)(2,1)}, u32[]{:S(2)}) copy-start(bf16[64,64]{0,1:T(8,128)(2,1)} %get-tuple-element.402) | copy-start | bytes 24580
  304.5 74.6 %copy-start.40 = (bf16[64,64]{0,1:T(8,128)(2,1)S(1)}, bf16[64,64]{0,1:T(8,128)(2,1)}, u32[]{:S(2)}) copy-start(bf16[64,64]{0,1:T(8,128)(2,1)} %get-tuple-element.411) | copy-start | bytes 24580
  304.5 74.8 %copy-start.35 = (bf16[64,64]{0,1:T(8,128)(2,1)S(1)}, bf16[64,64]{0,1:T(8,128)(2,1)}, u32[]{:S(2)}) copy-start(bf16[64,64]{0,1:T(8,128)(2,1)} %get-tuple-element.417) | copy-start | bytes 24580
  304.5 74.8 %copy-start.36 = (bf16[64,64]{0,1:T(8,128)(2,1)S(1)}, bf16[64,64]{0,1:T(8,128)(2,1)}, u32[]{:S(2)}) copy-start(bf16[64,64]{0,1:T(8,128)(2,1)} %get-tuple-element.419) | copy-start | bytes 24580
  304.5 75.0 %copy-start.37 = (bf16[64,64]{0,1:T(8,128)(2,1)S(1)}, bf16[64,64]{0,1:T(8,128)(2,1)}, u32[]{:S(2)}) copy-start(bf16[64,64]{0,1:T(8,128)(2,1)} %get-tuple-element.421) | copy-start | bytes 24580
  321.6 58.2 %copy-start.45 = (bf16[64,64]{0,1:T(8,128)(2,1)S(1)}, bf16[64,64]{0,1:T(8,128)(2,1)}, u32[]{:S(2)}) copy-start(bf16[64,64]{0,1:T(8,128)(2,1)} %get-tuple-element.395) | copy-start | bytes 24580
  321.6 58.2 %copy-start.46 = (bf16[64,64]{0,1:T(8,128)(2,1)S(1)}, bf16[64,64]{0,1:T(8,128)(2,1)}, u32[]{:S(2)}) copy-start(bf16[64,64]{0,1:T(8,128)(2,1)} %get-tuple-element.394) | copy-start | bytes 24580
  321.6 58.4 %copy-start.44 = (bf16[64,64]{0,1:T(8,128)(2,1)S(1)}, bf16[64,64]{0,1:T(8,128)(2,1)}, u32[]{:S(2)}) copy-start(bf16[64,64]{0,1:T(8,128)(2,1)} %get-tuple-element.396) | copy-start | bytes 24580
  321.7 58.6 %copy-start.29 = (bf16[64,64]{0,1:T(8,128)(2,1)S(1)}, bf16[64,64]{0,1:T(8,128)(2,1)}, u32[]{:S(2)}) copy-start(bf16[64,64]{0,1:T(8,128)(2,1)} %get-tuple-element.393) | copy-start | bytes 24580
  321.7 58.8 %copy-start.98 = (bf16[64,64]{0,1:T(8,128)(2,1)S(1)}, bf16[64,64]{0,1:T(8,128)(2,1)}, u32[]{:S(2)}) copy-start(bf16[64,64]{0,1:T(8,128)(2,1)} %get-tuple-element.386) | copy-start | bytes 24580
  321.7 58.8 %copy-start.104 = (bf16[64,64]{0,1:T(8,128)(2,1)S(1)}, bf16[64,64]{0,1:T(8,128)(2,1)}, u32[]{:S(2)}) copy-start(bf16[64,64]{0,1:T(8,128)(2,1)} %get-tuple-element.387) | copy-start | bytes 24580
  338.4 42.3 %copy-start.103 = (bf16[64,64]{0,1:T(8,128)(2,1)S(1)}, bf16[64,64]{0,1:T(8,128)(2,1)}, u32[]{:S(2)}) copy-start(bf16[64,64]{0,1:T(8,128)(2,1)} %get-tuple-element.388) | copy-start | bytes 24580
  338.4 42.5 %copy-start.102 = (bf16[64,64]{0,1:T(8,128)(2,1)S(1)}, bf16[64,64]{0,1:T(8,128)(2,1)}, u32[]{:S(2)}) copy-start(bf16[64,64]{0,1:T(8,128)(2,1)} %get-tuple-element.389) | copy-start | bytes 24580
  338.4 42.8 %copy-start.30 = (bf16[64,64]{0,1:T(8,128)(2,1)S(1)}, bf16[64,64]{0,1:T(8,128)(2,1)}, u32[]{:S(2)}) copy-start(bf16[64,64]{0,1:T(8,128)(2,1)} %get-tuple-element.398) | copy-start | bytes 24580
  372.4 23.3 %collective-permute-start.1 = (bf16[2,16,2048]{2,1,0:T(8,128)(2,1)S(1)}, bf16[2,16,2048]{2,1,0:T(8,128)(2,1)S(1)}, u32[]{:S(2)}, u32[]{:S(2)}) collective-permute-start(bf16[2,16,2048]{2,1,0:T(8,128)(2,1)S(1)} %slice.4455), channel_id=1, source_target_pairs={{8,0},{16,8},{24,16},{9,1},{17,9},{25,17},{10,2},{18,10},{26,18},{... | collective-permute-start | bytes 393224 | tf_op jit(solution)/shard_map/ppermute | solution.py:15
  374.4 25.8 %collective-permute-start.6 = (bf16[12,2,2048]{2,1,0:T(2,128)(2,1)}, bf16[12,2,2048]{2,1,0:T(2,128)(2,1)}, u32[]{:S(2)}, u32[]{:S(2)}) collective-permute-start(bf16[12,2,2048]{2,1,0:T(2,128)(2,1)} %get-tuple-element.506), channel_id=1, source_target_pairs={{0,1},{1,2},{2,3},{3,4},{4,5},{5,6},{6,7},{8,9},{9,10},{10,11},{11... | collective-permute-start | bytes 294920 | tf_op jit(solution)/shard_map/ppermute | solution.py:12
  391.3 12.0 %collective-permute-start.7 = (bf16[12,2,2048]{2,1,0:T(2,128)(2,1)}, bf16[12,2,2048]{2,1,0:T(2,128)(2,1)S(1)}, u32[]{:S(2)}, u32[]{:S(2)}) collective-permute-start(bf16[12,2,2048]{2,1,0:T(2,128)(2,1)} %get-tuple-element.507), channel_id=1, source_target_pairs={{1,0},{2,1},{3,2},{4,3},{5,4},{6,5},{7,6},{9,8},{10,9},{11,10},{12... | collective-permute-start | bytes 294920 | tf_op jit(solution)/shard_map/ppermute | solution.py:15
  396.7 56.8 %collective-permute-start.2 = (bf16[20,2,2048]{2,1,0:T(2,128)(2,1)}, bf16[20,2,2048]{2,1,0:T(2,128)(2,1)}, u32[]{:S(2)}, u32[]{:S(2)}) collective-permute-start(bf16[20,2,2048]{2,1,0:T(2,128)(2,1)} %get-tuple-element.342), channel_id=1, source_target_pairs={{0,1},{1,2},{2,3},{3,4},{4,5},{5,6},{6,7},{8,9},{9,10},{10,11},{11... | collective-permute-start | bytes 491528 | tf_op jit(solution)/shard_map/ppermute | solution.py:12
  400.1 53.4 %collective-permute-start.3 = (bf16[20,2,2048]{2,1,0:T(2,128)(2,1)}, bf16[20,2,2048]{2,1,0:T(2,128)(2,1)}, u32[]{:S(2)}, u32[]{:S(2)}) collective-permute-start(bf16[20,2,2048]{2,1,0:T(2,128)(2,1)} %get-tuple-element.343), channel_id=1, source_target_pairs={{1,0},{2,1},{3,2},{4,3},{5,4},{6,5},{7,6},{9,8},{10,9},{11,10},{12... | collective-permute-start | bytes 491528 | tf_op jit(solution)/shard_map/ppermute | solution.py:15
  435.8 122.5 %collective-permute-start.19 = (bf16[18,1,32,256]{3,2,1,0:T(8,128)(2,1)}, bf16[18,1,32,256]{3,2,1,0:T(8,128)(2,1)}, u32[]{:S(2)}, u32[]{:S(2)}) collective-permute-start(bf16[18,1,32,256]{3,2,1,0:T(8,128)(2,1)} %get-tuple-element.331), channel_id=1, source_target_pairs={{1,0},{2,1},{3,2},{4,3},{5,4},{6,5},{7,6},{9,8},{10,9},{11,10},{12... | collective-permute-start | bytes 884744 | tf_op jit(solution)/shard_map/ppermute | solution.py:15
  437.7 104.2 %collective-permute-start.18 = (bf16[18,1,32,256]{3,2,1,0:T(8,128)(2,1)}, bf16[18,1,32,256]{3,2,1,0:T(8,128)(2,1)}, u32[]{:S(2)}, u32[]{:S(2)}) collective-permute-start(bf16[18,1,32,256]{3,2,1,0:T(8,128)(2,1)} %get-tuple-element.332), channel_id=1, source_target_pairs={{0,1},{1,2},{2,3},{3,4},{4,5},{5,6},{6,7},{8,9},{9,10},{10,11},{11... | collective-permute-start | bytes 884744 | tf_op jit(solution)/shard_map/ppermute | solution.py:12
  (354 other events, 2194.3 us)
where the time goes:
time: 606 us; the launch traced here: 596 us
  matrix products  201 us (33%)
  other arithmetic  134 us (22%)
  local copies, waits for them, and re-layouts  125 us (21%)
  blocking collectives  66.2 us (11%)
  starting transfers between devices  58.9 us (10%)
  between operations  6.87 us (1%)
    another operation x16, other arithmetic, couple(): jnp.stack(totals[row_bit], axis=0)  119 us
    dot_general x9, matrix products, shards(): jnp.einsum('ijvs,ts->ijvt', neighbour, near_tiles[step_row * 3 + step_col...  71.2 us
    all_gather x1, blocking collectives, shards(): everything = lax.all_gather(flat_block, ('gx', 'gy'), axis=0, tiled=True)  66.2 us
    dot_general x71, matrix products, couple_one(): jnp.einsum('vr,sr->vs', window[code_row, code_col], coupling_block, prefe...  59.5 us
    dot_general x128, matrix products, couple(): jnp.einsum('pqvr,sr->pqvs', source, blocks, preferred_element_type=jnp.fl...  55.1 us
    slice x24, local copies, waits for them, and re-layouts, couple(): weight_mask = member[:, row_bit, :, col_bit, code_row * 6 + code_col]  39.7 us
    ppermute x10, starting transfers between devices, extended(): lax.ppermute(lax.slice_in_dim(block, 0, width, axis=dim), axis, backward)  32.1 us
    ppermute x10, starting transfers between devices, extended(): lax.ppermute(lax.slice_in_dim(block, block.shape[dim] - width, None, axis...  26.8 us
  transfers between devices with their start and end apart: 20, of which 3 were waited for; matrix products, arithmetic and copies ran while one was open for 67% of the time, Pallas kernels for 0%

commit v1 on v0

v1 whole, which is shorter than its diff:
```python
import functools

import jax
import jax.numpy as jnp
from jax import lax
from jax.experimental import pallas as pl
from jax.experimental.pallas import tpu as pltpu
from jax.sharding import PartitionSpec as P

MESH = pl.DeviceIdType.MESH
F32 = jnp.float32
BF16 = jnp.bfloat16
NT = (((1,), (1,)), ((), ()))
NN = (((1,), (0,)), ((), ()))
VMEM_LIMIT = 60 * 1024 * 1024
AXES = ("gx", "gy")
SIDES = [(sx, sy) for sx in (-1, 0, 1) for sy in (-1, 0, 1) if (sx, sy) != (0, 0)]


def dot(a, b, dims):
    return lax.dot_general(a, b, dims, preferred_element_type=F32)


def twice(matrix):
    return jnp.concatenate([matrix, matrix], axis=0)


def low_half(shape, rank):
    return lax.broadcasted_iota(jnp.int32, shape, len(shape) - 1) < rank


def pair_columns(wide, vectors, rank):
    pairs = wide.reshape(-1, 2, vectors, 2 * rank)
    even, odd = pairs[:, 0], pairs[:, 1]
    return jnp.where(low_half(even.shape, rank), even, odd).astype(BF16)


def split_columns(paired, rank):
    count, vectors, lanes = paired.shape
    low = low_half((1, lanes), rank).astype(F32).astype(BF16)
    both = jnp.stack([paired * low, paired * (1 - low)], axis=1)
    return both.reshape(count * 2 * vectors, lanes)


def up_kernel(levels, rank, samples, basis, transfer, *outs):
    patch, _, vectors, sources = samples.shape
    basis2 = twice(basis[...])

    def project(i, carry):
        rows = samples[i].reshape(patch * vectors, sources)
        outs[0][i] = pair_columns(dot(rows, basis2, NT), vectors, rank)
        return carry

    lax.fori_loop(0, patch, project, 0)
    for level in range(levels):
        child = outs[level]
        matrix = twice(transfer[level])
        for row in range(child.shape[0] // 2):
            grouped = jnp.concatenate([child[2 * row], child[2 * row + 1]], axis=-1)
            wide = dot(grouped.reshape(-1, 4 * rank), matrix, NT)
            if level < levels - 1:
                outs[level + 1][row] = pair_columns(wide, vectors, rank)
            else:
                odd = lax.axis_index("gy") % 2
                lane = lax.broadcasted_iota(jnp.int32, wide.shape, 1)
                own = (lane >= odd * rank) & (lane < (odd + 1) * rank)
                outs[level + 1][...] = jnp.where(own, wide, 0.0).astype(BF16)


def span(side, size, width):
    if side == 0:
        return pl.ds(0, size), pl.ds(width, size)
    if side > 0:
        return pl.ds(size - width, width), pl.ds(0, width)
    return pl.ds(0, width), pl.ds(width + size, width)


def exchange_kernel(widths, counts, *refs):
    blocks = len(widths)
    ins, top = refs[:blocks], refs[blocks]
    outs, top_out = refs[blocks + 1 : 2 * blocks + 1], refs[2 * blocks + 1]
    send, recv, local, top_send, top_recv = refs[2 * blocks + 2 :]
    across, along = counts
    total = across * along
    row, col = lax.axis_index("gx"), lax.axis_index("gy")
    me = row * along + col

    def place(device):
        return (device // along, device % along)

    barrier = pltpu.get_barrier_semaphore()

    def greet(step, carry):
        pl.semaphore_signal(
            barrier, inc=1, device_id=place((me + step) % total), device_id_type=MESH
        )
        return carry

    lax.fori_loop(1, total, greet, 0)
    pl.semaphore_wait(barrier, total - 1)

    def top_copy(step):
        return pltpu.make_async_remote_copy(
            src_ref=top,
            dst_ref=top_out.at[row, col],
            send_sem=top_send.at[step],
            recv_sem=top_recv.at[step],
            device_id=place((me + step) % total),
            device_id_type=MESH,
        )

    def start_top(step, carry):
        top_copy(step).start()
        return carry

    def side_copy(block, number):
        sx, sy = SIDES[number]
        source, target = ins[block], outs[block]
        wx, wy = widths[block]
        rows_from, rows_to = span(sx, source.shape[0], wx)
        cols_from, cols_to = span(sy, source.shape[1], wy)
        return pltpu.make_async_remote_copy(
            src_ref=source.at[rows_from, cols_from],
            dst_ref=target.at[rows_to, cols_to],
            send_sem=send.at[block, number],
            recv_sem=recv.at[block, number],
            device_id=(row + sx, col + sy),
            device_id_type=MESH,
        )

    def land(block, number):
        sx, sy = SIDES[number]
        source, target = ins[block], outs[block]
        wx, wy = widths[block]
        rows_from, rows_to = span(sx, source.shape[0], wx)
        cols_from, cols_to = span(sy, source.shape[1], wy)
        return pltpu.make_async_remote_copy(
            src_ref=source.at[rows_from, cols_from],
            dst_ref=target.at[rows_to, cols_to],
            send_sem=send.at[block, number],
            recv_sem=recv.at[block, number],
            device_id=(row - sx, col - sy),
            device_id_type=MESH,
        )

    def inside(sx, sy):
        there_row, there_col = row + sx, col + sy
        return (there_row >= 0) & (there_row < across) & (there_col >= 0) & (there_col < along)

    lax.fori_loop(1, total, start_top, 0)
    for number, (sx, sy) in enumerate(SIDES):

        @pl.when(inside(sx, sy))
        def _():
            for block in range(blocks):
                side_copy(block, number).start()

    own = []
    for block in range(blocks):
        wx, wy = widths[block]
        size_x, size_y = ins[block].shape[:2]
        copy = pltpu.make_async_copy(
            ins[block],
            outs[block].at[pl.ds(wx, size_x), pl.ds(wy, size_y)],
            local.at[block],
        )
        copy.start()
        own.append(copy)
    own_top = pltpu.make_async_copy(top, top_out.at[row, col], local.at[blocks])
    own_top.start()
    for copy in own:
        copy.wait()
    own_top.wait()
    for number, (sx, sy) in enumerate(SIDES):

        @pl.when(inside(-sx, -sy))
        def _():
            for block in range(blocks):
                land(block, number).wait_recv()

    def wait_top(step, carry):
        sender = (me + total - step) % total
        came = pltpu.make_async_remote_copy(
            src_ref=top,
            dst_ref=top_out.at[sender // along, sender % along],
            send_sem=top_send.at[step],
            recv_sem=top_recv.at[step],
            device_id=place(sender),
            device_id_type=MESH,
        )
        came.wait_recv()
        return carry

    lax.fori_loop(1, total, wait_top, 0)
    for block in range(blocks):
        target = outs[block]
        wx, wy = widths[block]
        rows, cols = target.shape[:2]
        for edge, spot in (
            (row == 0, (pl.ds(0, wx), pl.ds(0, cols))),
            (row == across - 1, (pl.ds(rows - wx, wx), pl.ds(0, cols))),
            (col == 0, (pl.ds(0, rows), pl.ds(0, wy))),
            (col == along - 1, (pl.ds(0, rows), pl.ds(cols - wy, wy))),
        ):

            @pl.when(edge)
            def _():
                shape = (spot[0].size, spot[1].size) + target.shape[2:]
                target[spot[0], spot[1]] = jnp.zeros(shape, target.dtype)

    for number, (sx, sy) in enumerate(SIDES):

        @pl.when(inside(sx, sy))
        def _():
            for block in range(blocks):
                side_copy(block, number).wait_send()

    def sent_top(step, carry):
        top_copy(step).wait_send()
        return carry

    lax.fori_loop(1, total, sent_top, 0)


def main_kernel(levels, rank, steps, offsets, *refs):
    padded_samples = refs[0]
    padded = refs[1 : 1 + levels]
    (tops, codes, codes_upper, basis, transfer, coupling, shifted, near, out) = refs[
        1 + levels : 10 + levels
    ]
    scratch = refs[10 + levels :]
    codes_flat, masks = scratch[0], scratch[1]
    uppers = scratch[2 : 2 + steps]
    downs = scratch[2 + steps :]
    patch, _, vectors, sources = out.shape
    across, along = tops.shape[:2]
    lanes = 2 * rank
    wide = 36 * rank
    row_index, col_index = lax.axis_index("gx"), lax.axis_index("gy")

    for level in range(levels):
        size = patch >> level
        for row in range(size):
            begin = (row << level) * patch * levels + level
            codes_flat[offsets[level] + row * size : offsets[level] + (row + 1) * size, :] = codes[
                pl.ds(begin, size, stride=levels << level), :
            ]
    codes_flat[offsets[levels] : offsets[levels] + codes_upper.shape[0], :] = codes_upper[...]
    code_lane = lax.broadcasted_iota(jnp.int32, (128, wide), 1) // rank
    code_row = lax.broadcasted_iota(jnp.int32, (128, wide), 0)
    widen = (code_lane == code_row).astype(F32).astype(BF16)
    group = 64

    def member(number, carry):
        start = pl.multiple_of(number * group, group)
        listed = codes_flat[pl.ds(start, group), :]
        code = lax.broadcasted_iota(jnp.int32, (group, 128), 1)
        found = jnp.zeros((group, 128), F32)
        for slot in range(listed.shape[1]):
            found = jnp.where(listed[:, slot : slot + 1] == code, 1.0, found)
        masks[pl.ds(start, group), :] = dot(found.astype(BF16), widen, NN)
        return carry

    lax.fori_loop(0, masks.shape[0] // group, member, 0)

    def weights(level, row_bit, col_bit):
        source = coupling if col_bit else shifted
        flat = jnp.concatenate(
            [source[level, code + 1 - row_bit, :, 0 : 6 * rank] for code in range(6)], axis=-1
        )
        return twice(flat)

    def window(ref, row, col):
        return jnp.concatenate(
            [ref[row + code, col + step] for code in range(6) for step in range(3)], axis=-1
        )

    def masked(slab, mask_row):
        mask = jnp.broadcast_to(masks[pl.ds(mask_row, 1), :], (16, wide)).astype(BF16)
        return (slab.reshape(-1, 16, wide) * mask[None]).reshape(slab.shape)

    uppers[0][...] = jnp.zeros(uppers[0].shape, BF16)
    for row in range(across):
        for col in range(along // 2):
            uppers[0][row + 2, col + 1] = tops[row, 2 * col] + tops[row, 2 * col + 1]
    top_matrix = twice(transfer[levels])
    for step in range(steps - 1):
        child, parent = uppers[step], uppers[step + 1]
        parent[...] = jnp.zeros(parent.shape, BF16)
        rows, cols = across >> step, along >> (step + 1)
        for row in range(rows // 2):
            grouped = jnp.concatenate(
                [child[2 * row + 2, 1 : 1 + cols], child[2 * row + 3, 1 : 1 + cols]], axis=-1
            )
            lifted = dot(grouped.reshape(-1, 4 * rank), top_matrix, NT)
            parent[row + 2, 1 : 1 + cols // 2] = pair_columns(lifted, vectors, rank)
    low = low_half((vectors, lanes), rank)
    low_mask = low_half((1, lanes), rank).astype(F32).astype(BF16)
    images = []
    begin = offsets[levels]
    for step in range(steps):
        rows, cols = across >> step, along >> step
        row, col = row_index // 2**step, col_index // 2**step
        slab = window(uppers[step], 2 * (row // 2), col // 2)
        slab = masked(slab, begin + row * cols + col)
        bit = row % 2
        image = []
        for source in (shifted, coupling):
            flat = jnp.concatenate(
                [source[levels, code + 1 - bit, :, 0 : 6 * rank] for code in range(6)], axis=-1
            )
            image.append(dot(slab, twice(flat), NT))
        images.append(jnp.where(col % 2 == 0, image[0], image[1]))
        begin += rows * cols
    down = images[-1]
    for step in range(steps - 2, -1, -1):
        row, col = row_index // 2**step, col_index // 2**step
        carried = dot(down.astype(BF16) * low_mask, top_matrix, NN)
        part = jnp.where(row % 2 == 0, carried[:, :lanes], carried[:, lanes:])
        turned = pltpu.roll(part, rank, 1)
        part = jnp.where(low == (col % 2 == 0), part, turned)
        down = images[step] + part
    spread_top = down.astype(BF16) * low_mask

    def level_row(level, row):
        size = patch >> level
        if level == levels - 1:
            parent = spread_top
        else:
            parent = split_columns(downs[level + 1][row], rank)
        carried = dot(parent, twice(transfer[level]), NN)
        slabs = [window(padded[level], 2 * row, col) for col in range(size // 2)]
        for row_bit in range(2):
            image = []
            for col_bit in range(2):
                start = offsets[level] + (2 * row + row_bit) * size + col_bit
                left = jnp.concatenate(
                    [masked(slabs[col], start + 2 * col) for col in range(size // 2)], axis=0
                )
                image.append(dot(left, weights(level, row_bit, col_bit), NT))
            total = jnp.where(low_half(image[0].shape, rank), image[0], image[1])
            total = total + carried[:, row_bit * lanes : (row_bit + 1) * lanes]
            downs[level][2 * row + row_bit] = total.astype(BF16).reshape(-1, vectors, lanes)

    for level in range(levels - 1, -1, -1):
        count = patch >> (level + 1)
        if count <= 2:
            for row in range(count):
                level_row(level, row)
        else:

            def body(row, carry, level=level):
                level_row(level, row)
                return carry

            lax.fori_loop(0, count, body, 0)

    near_flat = jnp.concatenate([near[number] for number in range(9)], axis=-1)
    basis2 = twice(basis[...])

    def finish(row, carry):
        left = jnp.concatenate(
            [
                padded_samples[row + step_row, step_col : step_col + patch].reshape(-1, sources)
                for step_row in range(3)
                for step_col in range(3)
            ],
            axis=-1,
        )
        total = dot(left, near_flat, NT)
        total = total + dot(split_columns(downs[0][row], rank), basis2, NN)
        out[row] = total.astype(BF16).reshape(patch, vectors, sources)
        return carry

    lax.fori_loop(0, patch, finish, 0)


def shards(
    samples,
    leaf_basis,
    transfer,
    coupling,
    near_tiles,
    codes_local,
    counts_local,
    codes_upper,
    counts_upper,
):
    patch, _, vectors, sources = samples.shape
    rank = leaf_basis.shape[0]
    levels = transfer.shape[0] - 1
    lanes = 2 * rank
    across, along = lax.axis_size("gx"), lax.axis_size("gy")
    steps = 1
    while across >> steps >= 2:
        steps += 1
    vmem = pl.BlockSpec(memory_space=pltpu.VMEM)

    slot = jnp.arange(codes_local.shape[-1], dtype=jnp.int32)
    listed = jnp.where(slot < counts_local[..., None], codes_local, -1)
    listed = listed.reshape(-1, codes_local.shape[-1])
    listed_upper = jnp.where(slot < counts_upper[..., None], codes_upper, -1)

    shapes = [
        jax.ShapeDtypeStruct((patch >> level, patch >> (level + 1), vectors, lanes), BF16)
        for level in range(levels)
    ]
    shapes.append(jax.ShapeDtypeStruct((vectors, lanes), BF16))
    coeffs = pl.pallas_call(
        functools.partial(up_kernel, levels, rank),
        out_shape=shapes,
        in_specs=[vmem] * 3,
        out_specs=[vmem] * len(shapes),
        compiler_params=pltpu.CompilerParams(vmem_limit_bytes=VMEM_LIMIT),
        name="up",
    )(samples, leaf_basis, transfer)

    blocks = [samples, *coeffs[:levels]]
    widths = [(1, 1)] + [(2, 1)] * levels
    padded_shapes = [
        jax.ShapeDtypeStruct(
            (block.shape[0] + 2 * wx, block.shape[1] + 2 * wy) + block.shape[2:], BF16
        )
        for block, (wx, wy) in zip(blocks, widths)
    ]
    padded_shapes.append(jax.ShapeDtypeStruct((across, along, vectors, lanes), BF16))
    total = across * along
    padded = pl.pallas_call(
        functools.partial(exchange_kernel, widths, (across, along)),
        out_shape=padded_shapes,
        in_specs=[vmem] * (len(blocks) + 1),
        out_specs=[vmem] * len(padded_shapes),
        scratch_shapes=[
            pltpu.SemaphoreType.DMA((len(blocks), len(SIDES))),
            pltpu.SemaphoreType.DMA((len(blocks), len(SIDES))),
            pltpu.SemaphoreType.DMA((len(blocks) + 1,)),
            pltpu.SemaphoreType.DMA((total,)),
            pltpu.SemaphoreType.DMA((total,)),
        ],
        compiler_params=pltpu.CompilerParams(
            collective_id=0, has_side_effects=True, vmem_limit_bytes=VMEM_LIMIT
        ),
        name="exchange",
    )(*blocks, coeffs[levels])

    offsets = [0]
    for level in range(levels):
        offsets.append(offsets[-1] + (patch >> level) ** 2)
    rows = offsets[-1] + codes_upper.shape[0]
    rows = (rows + 63) // 64 * 64
    shifted = coupling[..., rank:]
    return pl.pallas_call(
        functools.partial(main_kernel, levels, rank, steps, offsets),
        out_shape=jax.ShapeDtypeStruct(samples.shape, BF16),
        in_specs=[vmem] * (levels + 9),
        out_specs=vmem,
        scratch_shapes=[
            pltpu.VMEM((rows, codes_local.shape[-1]), jnp.int32),
            pltpu.VMEM((rows, 36 * rank), F32),
        ]
        + [
            pltpu.VMEM(((across >> step) + 4, (along >> (step + 1)) + 2, vectors, lanes), BF16)
            for step in range(steps)
        ]
        + [pltpu.VMEM(shape.shape, BF16) for shape in shapes[:levels]],
        compiler_params=pltpu.CompilerParams(vmem_limit_bytes=VMEM_LIMIT),
        name="finish",
    )(*padded, listed, listed_upper, leaf_basis, transfer, coupling, shifted, near_tiles)


def solution(mesh):
    placed = (
        P("gx", "gy", None, None),
        P(),
        P(),
        P(),
        P(),
        P("gx", "gy", None, None),
        P("gx", "gy", None),
        P(),
        P(),
    )
    return jax.shard_map(
        shards, mesh=mesh, in_specs=placed, out_specs=P("gx", "gy", None, None), check_vma=False
    )
```

time: 606 us -> 102 us (0.17)
  the two profiles are of different devices: /device:TPU:6 before, /device:TPU:5 now
where the time goes in v1:
time: 102 us; the launch traced here: 101 us
  Pallas kernels  93.9 us (92%)
  local copies, waits for them, and re-layouts  3.84 us (4%)
  other arithmetic  3.51 us (3%)
    pallas_call x1, Pallas kernels, shards(): pl.pallas_call(functools.partial(exchange_kernel, widths, (across, along)...  44.7 us
    pallas_call x1, Pallas kernels, shards(): pl.pallas_call(functools.partial(main_kernel, levels, rank, steps, offset...  41.9 us
    pallas_call x1, Pallas kernels, shards(): pl.pallas_call(functools.partial(up_kernel, levels, rank), out_shape=shap...  7.39 us
    select_n x1, other arithmetic, shards(): listed = jnp.where(slot < counts_local[..., None], codes_local, -1)  2.17 us
    slice x1, local copies, waits for them, and re-layouts, shards(): shifted = coupling[..., rank:]  2.12 us

profile of v1, /device:TPU:5, one launch (start us, length us, event | category | flops | bytes accessed | tf_op | source)
XLA Modules:
  0.0 101.3 jit_solution(15896737770716632646)
XLA Ops:
  0.0 0.8 copy.11
  0.8 1.3 %fusion.1.refs_7_ = s32[40,27]{1,0:T(8,128)} fusion(s32[40,27]{1,0:T(8,128)S(1)} %copy.11, s32[40]{0:T(128)} %param.17), kind=kLoop, calls=%fused_computation.3 | loop fusion | flops 2160 | bytes 8800 | tf_op jit(solution)/shard_map/jit(_where)/select_n | solution.py:402
  2.1 0.9 copy.10
  3.1 2.2 %fusion = s32[16,16,4,27]{3,2,1,0:T(4,128)} fusion(s32[16,16,4,27]{3,2,1,0:T(4,128)} %param.14, s32[16,16,4]{2,1,0:T(8,128)S(1)} %copy.10), kind=kLoop, calls=%fused_computation.1 | loop fusion | flops 55296 | bytes 225280 | tf_op jit(solution)/shard_map/jit(_where)/select_n | solution.py:400
  5.2 0.0 copy-start
  5.2 7.4 %up.1 = (bf16[16,8,32,128]{3,2,1,0:T(8,128)(2,1)}, bf16[8,4,32,128]{3,2,1,0:T(8,128)(2,1)}, bf16[4,2,32,128]{3,2,1,0:T(8,128)(2,1)}, bf16[2,1,32,128]{3,2,1,0:T(8,128)(2,1)}, bf16[32,128]{1,0:T(8,128)(2,1)}) custom-call(bf16[16,16,32,256]{3,2,1,0:T(8,128)(2,1)} %refs_0_.1, bf16[64,256]{1,0:T(8,128)(2,1)} %refs_8_.1, bf16[5,64,256]{2,1,0:T(8,128)(2,1)} %refs_9_.1), custom_call_target="tpu_custom_call" | custom-call | tf_op jit(solution)/shard_map/up/pallas_call | solution.py:409
  12.6 0.0 copy-done
  12.6 2.1 %slice.3.refs_11_ = bf16[5,7,64,384]{3,2,1,0:T(8,128)(2,1)} slice(bf16[5,7,64,448]{3,2,1,0:T(8,128)(2,1)S(1)} %copy-done), slice={[0:5], [0:7], [0:64], [64:448]} | slice | bytes 3440640 | tf_op jit(solution)/shard_map/slice | solution.py:451
  14.7 44.7 %exchange.1 = (bf16[18,18,32,256]{3,2,1,0:T(8,128)(2,1)}, bf16[20,10,32,128]{3,2,1,0:T(8,128)(2,1)}, bf16[12,6,32,128]{3,2,1,0:T(8,128)(2,1)}, bf16[8,4,32,128]{...) custom-call(bf16[16,16,32,256]{3,2,1,0:T(8,128)(2,1)} %refs_0_.1, ...), custom_call_target="tpu_custom_call" | custom-call | tf_op jit(solution)/shard_map/exchange/pallas_call | solution.py:428
  59.4 41.9 %finish.1 = bf16[16,16,32,256]{3,2,1,0:T(8,128)(2,1)} custom-call(bf16[18,18,32,256]{3,2,1,0:T(8,128)(2,1)} %get-tuple-element.21.refs_0_, bf16[20,10,32,128]{3,2,1,0:T(8,128)(2,1)} %get-tuple-element.22.refs_1_, bf16[12,6,32,128]{3,2,1,0:T(8,128)(2,1)} %get-tuple-element.23.refs_2_, bf16[8,4,32,128]{3,2,1,0:T(8,128)(2,1)} %get-tuple-element.24.refs_3_, ...), custom_call_target="tpu_custom_call" | custom-call | tf_op jit(solution)/shard_map/finish/pallas_call | solution.py:452
Async XLA Ops:
  5.2 7.4 %copy-start = (bf16[5,7,64,448]{3,2,1,0:T(8,128)(2,1)S(1)}, bf16[5,7,64,448]{3,2,1,0:T(8,128)(2,1)}, u32[]{:S(2)}) copy-start(bf16[5,7,64,448]{3,2,1,0:T(8,128)(2,1)} %refs_10_.1) | copy-start | bytes 6021124

commit v2 on v1

--- a/solution.py
+++ b/solution.py
@@ -75,15 +75,40 @@
     return pl.ds(0, width), pl.ds(width + size, width)
 
 
-def exchange_kernel(widths, counts, *refs):
-    blocks = len(widths)
-    ins, top = refs[:blocks], refs[blocks]
-    outs, top_out = refs[blocks + 1 : 2 * blocks + 1], refs[2 * blocks + 1]
-    send, recv, local, top_send, top_recv = refs[2 * blocks + 2 :]
+def main_kernel(levels, rank, steps, offsets, counts, *refs):
+    samples = refs[0]
+    coeffs = refs[1 : 1 + levels]
+    (top, codes, codes_upper, basis, transfer, coupling, shifted, near, out) = refs[
+        1 + levels : 10 + levels
+    ]
+    scratch = refs[10 + levels :]
+    codes_flat, masks, tops, total_near, top_rim, bottom_rim, left_rim, right_rim = scratch[:8]
+    send, recv, local, top_send, top_recv = scratch[8:13]
+    padded = scratch[13 : 13 + levels]
+    uppers = scratch[13 + levels : 13 + levels + steps]
+    downs = scratch[13 + levels + steps :]
+    patch, _, vectors, sources = out.shape
     across, along = counts
     total = across * along
-    row, col = lax.axis_index("gx"), lax.axis_index("gy")
-    me = row * along + col
+    lanes = 2 * rank
+    wide = 36 * rank
+    row_index, col_index = lax.axis_index("gx"), lax.axis_index("gy")
+    me = row_index * along + col_index
+
+    for rim in (top_rim, bottom_rim, left_rim, right_rim):
+        rim[...] = jnp.zeros(rim.shape, BF16)
+    for level in range(levels):
+        target = padded[level]
+        rows, cols = target.shape[:2]
+        for spot in (
+            (pl.ds(0, 2), pl.ds(0, cols)),
+            (pl.ds(rows - 2, 2), pl.ds(0, cols)),
+            (pl.ds(2, rows - 4), pl.ds(0, 1)),
+            (pl.ds(2, rows - 4), pl.ds(cols - 1, 1)),
+        ):
+            target[spot[0], spot[1]] = jnp.zeros(
+                (spot[0].size, spot[1].size, vectors, lanes), BF16
+            )
 
     def place(device):
         return (device // along, device % along)
@@ -97,146 +122,69 @@
         return carry
 
     lax.fori_loop(1, total, greet, 0)
-    pl.semaphore_wait(barrier, total - 1)
-
-    def top_copy(step):
+
+    def top_copy(step, sender):
         return pltpu.make_async_remote_copy(
             src_ref=top,
-            dst_ref=top_out.at[row, col],
+            dst_ref=tops.at[sender // along, sender % along],
             send_sem=top_send.at[step],
             recv_sem=top_recv.at[step],
             device_id=place((me + step) % total),
             device_id_type=MESH,
         )
 
-    def start_top(step, carry):
-        top_copy(step).start()
-        return carry
-
-    def side_copy(block, number):
+    def coeff_copy(level, number):
         sx, sy = SIDES[number]
-        source, target = ins[block], outs[block]
-        wx, wy = widths[block]
-        rows_from, rows_to = span(sx, source.shape[0], wx)
-        cols_from, cols_to = span(sy, source.shape[1], wy)
+        size_x, size_y = coeffs[level].shape[:2]
+        rows_from, rows_to = span(sx, size_x, 2)
+        cols_from, cols_to = span(sy, size_y, 1)
         return pltpu.make_async_remote_copy(
-            src_ref=source.at[rows_from, cols_from],
-            dst_ref=target.at[rows_to, cols_to],
-            send_sem=send.at[block, number],
-            recv_sem=recv.at[block, number],
-            device_id=(row + sx, col + sy),
+            src_ref=coeffs[level].at[rows_from, cols_from],
+            dst_ref=padded[level].at[rows_to, cols_to],
+            send_sem=send.at[level, number],
+            recv_sem=recv.at[level, number],
+            device_id=(row_index + sx, col_index + sy),
             device_id_type=MESH,
         )
 
-    def land(block, number):
+    def sample_copy(number):
         sx, sy = SIDES[number]
-        source, target = ins[block], outs[block]
-        wx, wy = widths[block]
-        rows_from, rows_to = span(sx, source.shape[0], wx)
-        cols_from, cols_to = span(sy, source.shape[1], wy)
+        rows_from, _ = span(sx, patch, 1)
+        cols_from, cols_to = span(sy, patch, 1)
+        if sx == 0:
+            rim = left_rim if sy > 0 else right_rim
+            spot = rim.at[pl.ds(1, patch), pl.ds(0, 1)]
+        else:
+            rim = top_rim if sx > 0 else bottom_rim
+            spot = rim.at[pl.ds(0, 1), cols_to]
         return pltpu.make_async_remote_copy(
-            src_ref=source.at[rows_from, cols_from],
-            dst_ref=target.at[rows_to, cols_to],
-            send_sem=send.at[block, number],
-            recv_sem=recv.at[block, number],
-            device_id=(row - sx, col - sy),
+            src_ref=samples.at[rows_from, cols_from],
+            dst_ref=spot,
+            send_sem=send.at[levels, number],
+            recv_sem=recv.at[levels, number],
+            device_id=(row_index + sx, col_index + sy),
             device_id_type=MESH,
         )
 
     def inside(sx, sy):
-        there_row, there_col = row + sx, col + sy
+        there_row, there_col = row_index + sx, col_index + sy
         return (there_row >= 0) & (there_row < across) & (there_col >= 0) & (there_col < along)
 
-    lax.fori_loop(1, total, start_top, 0)
-    for number, (sx, sy) in enumerate(SIDES):
-
-        @pl.when(inside(sx, sy))
-        def _():
-            for block in range(blocks):
-                side_copy(block, number).start()
-
-    own = []
-    for block in range(blocks):
-        wx, wy = widths[block]
-        size_x, size_y = ins[block].shape[:2]
-        copy = pltpu.make_async_copy(
-            ins[block],
-            outs[block].at[pl.ds(wx, size_x), pl.ds(wy, size_y)],
-            local.at[block],
-        )
+    own = [
+        pltpu.make_async_copy(
+            coeffs[level],
+            padded[level].at[
+                pl.ds(2, coeffs[level].shape[0]), pl.ds(1, coeffs[level].shape[1])
+            ],
+            local.at[level],
+        )
+        for level in range(levels)
+    ]
+    own.append(
+        pltpu.make_async_copy(top, tops.at[row_index, col_index], local.at[levels])
+    )
+    for copy in own:
         copy.start()
-        own.append(copy)
-    own_top = pltpu.make_async_copy(top, top_out.at[row, col], local.at[blocks])
-    own_top.start()
-    for copy in own:
-        copy.wait()
-    own_top.wait()
-    for number, (sx, sy) in enumerate(SIDES):
-
-        @pl.when(inside(-sx, -sy))
-        def _():
-            for block in range(blocks):
-                land(block, number).wait_recv()
-
-    def wait_top(step, carry):
-        sender = (me + total - step) % total
-        came = pltpu.make_async_remote_copy(
-            src_ref=top,
-            dst_ref=top_out.at[sender // along, sender % along],
-            send_sem=top_send.at[step],
-            recv_sem=top_recv.at[step],
-            device_id=place(sender),
-            device_id_type=MESH,
-        )
-        came.wait_recv()
-        return carry
-
-    lax.fori_loop(1, total, wait_top, 0)
-    for block in range(blocks):
-        target = outs[block]
-        wx, wy = widths[block]
-        rows, cols = target.shape[:2]
-        for edge, spot in (
-            (row == 0, (pl.ds(0, wx), pl.ds(0, cols))),
-            (row == across - 1, (pl.ds(rows - wx, wx), pl.ds(0, cols))),
-            (col == 0, (pl.ds(0, rows), pl.ds(0, wy))),
-            (col == along - 1, (pl.ds(0, rows), pl.ds(cols - wy, wy))),
-        ):
-
-            @pl.when(edge)
-            def _():
-                shape = (spot[0].size, spot[1].size) + target.shape[2:]
-                target[spot[0], spot[1]] = jnp.zeros(shape, target.dtype)
-
-    for number, (sx, sy) in enumerate(SIDES):
-
-        @pl.when(inside(sx, sy))
-        def _():
-            for block in range(blocks):
-                side_copy(block, number).wait_send()
-
-    def sent_top(step, carry):
-        top_copy(step).wait_send()
-        return carry
-
-    lax.fori_loop(1, total, sent_top, 0)
-
-
-def main_kernel(levels, rank, steps, offsets, *refs):
-    padded_samples = refs[0]
-    padded = refs[1 : 1 + levels]
-    (tops, codes, codes_upper, basis, transfer, coupling, shifted, near, out) = refs[
-        1 + levels : 10 + levels
-    ]
-    scratch = refs[10 + levels :]
-    codes_flat, masks = scratch[0], scratch[1]
-    uppers = scratch[2 : 2 + steps]
-    downs = scratch[2 + steps :]
-    patch, _, vectors, sources = out.shape
-    across, along = tops.shape[:2]
-    lanes = 2 * rank
-    wide = 36 * rank
-    row_index, col_index = lax.axis_index("gx"), lax.axis_index("gy")
 
     for level in range(levels):
         size = patch >> level
@@ -262,6 +210,64 @@
         return carry
 
     lax.fori_loop(0, masks.shape[0] // group, member, 0)
+
+    pl.semaphore_wait(barrier, total - 1)
+
+    def start_top(step, carry):
+        top_copy(step, me).start()
+        return carry
+
+    lax.fori_loop(1, total, start_top, 0)
+    for number, (sx, sy) in enumerate(SIDES):
+
+        @pl.when(inside(sx, sy))
+        def _():
+            for level in range(levels):
+                coeff_copy(level, number).start()
+
+    for number, (sx, sy) in enumerate(SIDES):
+
+        @pl.when(inside(sx, sy))
+        def _():
+            sample_copy(number).start()
+
+    def near_row(row, row_steps):
+        blank = jnp.zeros((1, vectors, sources), BF16)
+        left = []
+        for row_step in row_steps:
+            line = samples[row + row_step - 1]
+            left.append(jnp.concatenate([blank, line[: patch - 1]], axis=0))
+            left.append(line)
+            left.append(jnp.concatenate([line[1:], blank], axis=0))
+        left = jnp.concatenate([part.reshape(-1, sources) for part in left], axis=-1)
+        flat = jnp.concatenate(
+            [near[3 * row_step + step] for row_step in row_steps for step in range(3)], axis=-1
+        )
+        total_near[row] = dot(left, flat, NT)
+
+    near_row(0, (1, 2))
+    near_row(patch - 1, (0, 1))
+
+    def near_body(row, carry):
+        near_row(row, (0, 1, 2))
+        return carry
+
+    lax.fori_loop(1, patch - 1, near_body, 0)
+
+    for copy in own:
+        copy.wait()
+    for number, (sx, sy) in enumerate(SIDES):
+
+        @pl.when(inside(-sx, -sy))
+        def _():
+            for level in range(levels):
+                coeff_copy(level, number).wait_recv()
+
+    def wait_top(step, carry):
+        top_copy(step, (me + total - step) % total).wait_recv()
+        return carry
+
+    lax.fori_loop(1, total, wait_top, 0)
 
     def weights(level, row_bit, col_bit):
         source = coupling if col_bit else shifted
@@ -355,24 +361,48 @@
 
             lax.fori_loop(0, count, body, 0)
 
-    near_flat = jnp.concatenate([near[number] for number in range(9)], axis=-1)
+    for number, (sx, sy) in enumerate(SIDES):
+
+        @pl.when(inside(-sx, -sy))
+        def _():
+            sample_copy(number).wait_recv()
+
+    for rim, column, step in ((left_rim, 0, 0), (right_rim, patch - 1, 2)):
+        left = jnp.concatenate(
+            [rim[part : part + patch, 0].reshape(-1, sources) for part in range(3)], axis=-1
+        )
+        flat = jnp.concatenate([near[3 * part + step] for part in range(3)], axis=-1)
+        extra = dot(left, flat, NT).reshape(patch, vectors, sources)
+        spot = pl.ds(column * vectors, vectors)
+        total_near[:, spot, :] = total_near[:, spot, :] + extra
+    for rim, row, step in ((top_rim, 0, 0), (bottom_rim, patch - 1, 6)):
+        left = jnp.concatenate(
+            [rim[0, part : part + patch].reshape(-1, sources) for part in range(3)], axis=-1
+        )
+        flat = jnp.concatenate([near[step + part] for part in range(3)], axis=-1)
+        total_near[row] = total_near[row] + dot(left, flat, NT)
     basis2 = twice(basis[...])
 
     def finish(row, carry):
-        left = jnp.concatenate(
-            [
-                padded_samples[row + step_row, step_col : step_col + patch].reshape(-1, sources)
-                for step_row in range(3)
-                for step_col in range(3)
-            ],
-            axis=-1,
-        )
-        total = dot(left, near_flat, NT)
-        total = total + dot(split_columns(downs[0][row], rank), basis2, NN)
-        out[row] = total.astype(BF16).reshape(patch, vectors, sources)
+        summed = total_near[row] + dot(split_columns(downs[0][row], rank), basis2, NN)
+        out[row] = summed.astype(BF16).reshape(patch, vectors, sources)
         return carry
 
     lax.fori_loop(0, patch, finish, 0)
+
+    for number, (sx, sy) in enumerate(SIDES):
+
+        @pl.when(inside(sx, sy))
+        def _():
+            for level in range(levels):
+                coeff_copy(level, number).wait_send()
+            sample_copy(number).wait_send()
+
+    def sent_top(step, carry):
+        top_copy(step, me).wait_send()
+        return carry
+
+    lax.fori_loop(1, total, sent_top, 0)
 
 
 def shards(
@@ -415,34 +445,6 @@
         name="up",
     )(samples, leaf_basis, transfer)
 
-    blocks = [samples, *coeffs[:levels]]
-    widths = [(1, 1)] + [(2, 1)] * levels
-    padded_shapes = [
-        jax.ShapeDtypeStruct(
-            (block.shape[0] + 2 * wx, block.shape[1] + 2 * wy) + block.shape[2:], BF16
-        )
-        for block, (wx, wy) in zip(blocks, widths)
-    ]
-    padded_shapes.append(jax.ShapeDtypeStruct((across, along, vectors, lanes), BF16))
-    total = across * along
-    padded = pl.pallas_call(
-        functools.partial(exchange_kernel, widths, (across, along)),
-        out_shape=padded_shapes,
-        in_specs=[vmem] * (len(blocks) + 1),
-        out_specs=[vmem] * len(padded_shapes),
-        scratch_shapes=[
-            pltpu.SemaphoreType.DMA((len(blocks), len(SIDES))),
-            pltpu.SemaphoreType.DMA((len(blocks), len(SIDES))),
-            pltpu.SemaphoreType.DMA((len(blocks) + 1,)),
-            pltpu.SemaphoreType.DMA((total,)),
-            pltpu.SemaphoreType.DMA((total,)),
-        ],
-        compiler_params=pltpu.CompilerParams(
-            collective_id=0, has_side_effects=True, vmem_limit_bytes=VMEM_LIMIT
-        ),
-        name="exchange",
-    )(*blocks, coeffs[levels])
-
     offsets = [0]
     for level in range(levels):
         offsets.append(offsets[-1] + (patch >> level) ** 2)
@@ -450,22 +452,39 @@
     rows = (rows + 63) // 64 * 64
     shifted = coupling[..., rank:]
     return pl.pallas_call(
-        functools.partial(main_kernel, levels, rank, steps, offsets),
+        functools.partial(main_kernel, levels, rank, steps, offsets, (across, along)),
         out_shape=jax.ShapeDtypeStruct(samples.shape, BF16),
-        in_specs=[vmem] * (levels + 9),
+        in_specs=[vmem] * (levels + 10 - 1),
         out_specs=vmem,
         scratch_shapes=[
             pltpu.VMEM((rows, codes_local.shape[-1]), jnp.int32),
             pltpu.VMEM((rows, 36 * rank), F32),
+            pltpu.VMEM((across, along, vectors, lanes), BF16),
+            pltpu.VMEM((patch, patch * vectors, sources), F32),
+            pltpu.VMEM((1, patch + 2, vectors, sources), BF16),
+            pltpu.VMEM((1, patch + 2, vectors, sources), BF16),
+            pltpu.VMEM((patch + 2, 1, vectors, sources), BF16),
+            pltpu.VMEM((patch + 2, 1, vectors, sources), BF16),
+            pltpu.SemaphoreType.DMA((levels + 1, len(SIDES))),
+            pltpu.SemaphoreType.DMA((levels + 1, len(SIDES))),
+            pltpu.SemaphoreType.DMA((levels + 1,)),
+            pltpu.SemaphoreType.DMA((across * along,)),
+            pltpu.SemaphoreType.DMA((across * along,)),
+        ]
+        + [
+            pltpu.VMEM((shape.shape[0] + 4, shape.shape[1] + 2, vectors, lanes), BF16)
+            for shape in shapes[:levels]
         ]
         + [
             pltpu.VMEM(((across >> step) + 4, (along >> (step + 1)) + 2, vectors, lanes), BF16)
             for step in range(steps)
         ]
         + [pltpu.VMEM(shape.shape, BF16) for shape in shapes[:levels]],
-        compiler_params=pltpu.CompilerParams(vmem_limit_bytes=VMEM_LIMIT),
+        compiler_params=pltpu.CompilerParams(
+            collective_id=0, has_side_effects=True, vmem_limit_bytes=VMEM_LIMIT
+        ),
         name="finish",
-    )(*padded, listed, listed_upper, leaf_basis, transfer, coupling, shifted, near_tiles)
+    )(samples, *coeffs, listed, listed_upper, leaf_basis, transfer, coupling, shifted, near_tiles)
 
 
 def solution(mesh):

time: 102 us -> 82.1 us (0.80)
  Pallas kernels: 93.9 us -> 69.5 us
  local copies, waits for them, and re-layouts: 3.84 us -> 8.74 us
    pallas_call x1 -> x0, Pallas kernels: 44.7 us -> none  [shards(): pl.pallas_call(functools.partial(exchange_kernel, widths, (across, along)...]
    pallas_call x1, Pallas kernels: 41.9 us -> 62.2 us  [shards(): pl.pallas_call(functools.partial(main_kernel, levels, rank, steps, offset...]
    unnamed x4 -> x5, local copies, waits for them, and re-layouts: 1.72 us -> 6.67 us
where the time goes in v2:
time: 82.1 us; the launch traced here: 81.8 us
  Pallas kernels  69.5 us (85%)
  local copies, waits for them, and re-layouts  8.74 us (11%)
  other arithmetic  3.52 us (4%)
    pallas_call x1, Pallas kernels, shards(): pl.pallas_call(functools.partial(main_kernel, levels, rank, steps, offset...  62.2 us
    pallas_call x1, Pallas kernels, shards(): pl.pallas_call(functools.partial(up_kernel, levels, rank), out_shape=shap...  7.25 us
    unnamed x5, local copies, waits for them, and re-layouts  6.67 us
    select_n x1, other arithmetic, shards(): listed = jnp.where(slot < counts_local[..., None], codes_local, -1)  2.19 us
    slice x1, local copies, waits for them, and re-layouts, shards(): shifted = coupling[..., rank:]  2.07 us

profile of v2, /device:TPU:5, one launch (start us, length us, event | category | flops | bytes accessed | tf_op | source)
XLA Modules:
  0.0 81.8 jit_solution(3601759435732584203)
XLA Ops:
  0.0 0.0 copy-start
  0.0 0.9 %copy.11 = s32[40,27]{1,0:T(8,128)S(1)} copy(s32[40,27]{0,1:T(8,128)} %param.16) | data formatting | bytes 8640 | tf_op args[7]
  0.9 1.3 %fusion.1.refs_7_ = s32[40,27]{1,0:T(8,128)} fusion(s32[40,27]{1,0:T(8,128)S(1)} %copy.11, s32[40]{0:T(128)} %param.17), kind=kLoop, calls=%fused_computation.3 | loop fusion | flops 2160 | bytes 8800 | tf_op jit(solution)/shard_map/jit(_where)/select_n | solution.py:432
  2.3 0.9 %copy.10 = s32[16,16,4]{2,1,0:T(8,128)S(1)} copy(s32[16,16,4]{1,2,0:T(4,128)} %param.15) | data formatting | bytes 8192 | tf_op args[6]
  3.2 2.2 %fusion = s32[16,16,4,27]{3,2,1,0:T(4,128)} fusion(s32[16,16,4,27]{3,2,1,0:T(4,128)} %param.14, s32[16,16,4]{2,1,0:T(8,128)S(1)} %copy.10), kind=kLoop, calls=%fused_computation.1 | loop fusion | flops 55296 | bytes 225280 | tf_op jit(solution)/shard_map/jit(_where)/select_n | solution.py:430
  5.4 7.2 %up.1 = (bf16[16,8,32,128]{3,2,1,0:T(8,128)(2,1)}, bf16[8,4,32,128]{3,2,1,0:T(8,128)(2,1)}, bf16[4,2,32,128]{3,2,1,0:T(8,128)(2,1)}, bf16[2,1,32,128]{3,2,1,0:T(8,128)(2,1)}, bf16[32,128]{1,0:T(8,128)(2,1)}) custom-call(bf16[16,16,32,256]{3,2,1,0:T(8,128)(2,1)} %refs_0_.1, bf16[64,256]{1,0:T(8,128)(2,1)} %refs_8_.1, bf16[5,64,256]{2,1,0:T(8,128)(2,1)} %refs_9_.1), custom_call_target="tpu_custom_call" | custom-call | tf_op jit(solution)/shard_map/up/pallas_call | solution.py:439
  12.6 0.0 copy-done
  12.6 2.1 %slice.3.refs_11_ = bf16[5,7,64,384]{3,2,1,0:T(8,128)(2,1)} slice(bf16[5,7,64,448]{3,2,1,0:T(8,128)(2,1)S(1)} %copy-done), slice={[0:5], [0:7], [0:64], [64:448]} | slice | bytes 3440640 | tf_op jit(solution)/shard_map/slice | solution.py:453
  14.7 62.2 %finish.1 = bf16[16,16,32,256]{3,2,1,0:T(8,128)(2,1)} custom-call(bf16[16,16,32,256]{3,2,1,0:T(8,128)(2,1)} %refs_0_.1, bf16[16,8,32,128]{3,2,1,0:T(8,128)(2,1)} %get-tuple-element.10.refs_1_, bf16[8,4,32,128]{3,2,1,0:T(8,128)(2,1)} %get-tuple-element.11.refs_2_, bf16[4,2,32,128]{3,2,1,0:T(8,128)(2,1)} %get-tuple-element.12.refs_3_, ...), custom_call_target="tpu_custom_call" | custom-call | tf_op jit(solution)/shard_map/finish/pallas_call | solution.py:454
  77.0 4.8 %copy.13 = bf16[16,16,32,256]{3,2,1,0:T(8,128)(2,1)} copy(bf16[16,16,32,256]{3,2,1,0:T(8,128)(2,1)} %finish.1) | data formatting | bytes 8388608
Async XLA Ops:
  0.0 12.6 %copy-start = (bf16[5,7,64,448]{3,2,1,0:T(8,128)(2,1)S(1)}, bf16[5,7,64,448]{3,2,1,0:T(8,128)(2,1)}, u32[]{:S(2)}) copy-start(bf16[5,7,64,448]{3,2,1,0:T(8,128)(2,1)} %refs_10_.1) | copy-start | bytes 6021124

commit v3 on v2

--- a/solution.py
+++ b/solution.py
@@ -42,31 +42,6 @@
     return both.reshape(count * 2 * vectors, lanes)
 
 
-def up_kernel(levels, rank, samples, basis, transfer, *outs):
-    patch, _, vectors, sources = samples.shape
-    basis2 = twice(basis[...])
-
-    def project(i, carry):
-        rows = samples[i].reshape(patch * vectors, sources)
-        outs[0][i] = pair_columns(dot(rows, basis2, NT), vectors, rank)
-        return carry
-
-    lax.fori_loop(0, patch, project, 0)
-    for level in range(levels):
-        child = outs[level]
-        matrix = twice(transfer[level])
-        for row in range(child.shape[0] // 2):
-            grouped = jnp.concatenate([child[2 * row], child[2 * row + 1]], axis=-1)
-            wide = dot(grouped.reshape(-1, 4 * rank), matrix, NT)
-            if level < levels - 1:
-                outs[level + 1][row] = pair_columns(wide, vectors, rank)
-            else:
-                odd = lax.axis_index("gy") % 2
-                lane = lax.broadcasted_iota(jnp.int32, wide.shape, 1)
-                own = (lane >= odd * rank) & (lane < (odd + 1) * rank)
-                outs[level + 1][...] = jnp.where(own, wide, 0.0).astype(BF16)
-
-
 def span(side, size, width):
     if side == 0:
         return pl.ds(0, size), pl.ds(width, size)
@@ -76,14 +51,11 @@
 
 
 def main_kernel(levels, rank, steps, offsets, counts, *refs):
-    samples = refs[0]
-    coeffs = refs[1 : 1 + levels]
-    (top, codes, codes_upper, basis, transfer, coupling, shifted, near, out) = refs[
-        1 + levels : 10 + levels
-    ]
-    scratch = refs[10 + levels :]
+    (samples, codes, listed_counts, codes_upper, counts_upper) = refs[:5]
+    (basis, transfer, coupling, near, out) = refs[5:10]
+    scratch = refs[10:]
     codes_flat, masks, tops, total_near, top_rim, bottom_rim, left_rim, right_rim = scratch[:8]
-    send, recv, local, top_send, top_recv = scratch[8:13]
+    send, recv, shifted, top_send, top_recv = scratch[8:13]
     padded = scratch[13 : 13 + levels]
     uppers = scratch[13 + levels : 13 + levels + steps]
     downs = scratch[13 + levels + steps :]
@@ -125,7 +97,7 @@
 
     def top_copy(step, sender):
         return pltpu.make_async_remote_copy(
-            src_ref=top,
+            src_ref=tops.at[row_index, col_index],
             dst_ref=tops.at[sender // along, sender % along],
             send_sem=top_send.at[step],
             recv_sem=top_recv.at[step],
@@ -135,11 +107,12 @@
 
     def coeff_copy(level, number):
         sx, sy = SIDES[number]
-        size_x, size_y = coeffs[level].shape[:2]
-        rows_from, rows_to = span(sx, size_x, 2)
-        cols_from, cols_to = span(sy, size_y, 1)
+        rows_from, rows_to = span(sx, patch >> level, 2)
+        cols_from, cols_to = span(sy, patch >> (level + 1), 1)
+        rows_from = pl.ds(rows_from.start + 2, rows_from.size)
+        cols_from = pl.ds(cols_from.start + 1, cols_from.size)
         return pltpu.make_async_remote_copy(
-            src_ref=coeffs[level].at[rows_from, cols_from],
+            src_ref=padded[level].at[rows_from, cols_from],
             dst_ref=padded[level].at[rows_to, cols_to],
             send_sem=send.at[level, number],
             recv_sem=recv.at[level, number],
@@ -147,21 +120,24 @@
             device_id_type=MESH,
         )
 
-    def sample_copy(number):
+    half = patch // 2
+
+    def sample_copy(number, late=False):
         sx, sy = SIDES[number]
         rows_from, _ = span(sx, patch, 1)
         cols_from, cols_to = span(sy, patch, 1)
         if sx == 0:
             rim = left_rim if sy > 0 else right_rim
-            spot = rim.at[pl.ds(1, patch), pl.ds(0, 1)]
+            rows_from = pl.ds(half if late else 0, half)
+            spot = rim.at[pl.ds(1 + rows_from.start, half), pl.ds(0, 1)]
         else:
             rim = top_rim if sx > 0 else bottom_rim
             spot = rim.at[pl.ds(0, 1), cols_to]
         return pltpu.make_async_remote_copy(
             src_ref=samples.at[rows_from, cols_from],
             dst_ref=spot,
-            send_sem=send.at[levels, number],
-            recv_sem=recv.at[levels, number],
+            send_sem=send.at[levels + late, number],
+            recv_sem=recv.at[levels + late, number],
             device_id=(row_index + sx, col_index + sy),
             device_id_type=MESH,
         )
@@ -170,30 +146,24 @@
         there_row, there_col = row_index + sx, col_index + sy
         return (there_row >= 0) & (there_row < across) & (there_col >= 0) & (there_col < along)
 
-    own = [
-        pltpu.make_async_copy(
-            coeffs[level],
-            padded[level].at[
-                pl.ds(2, coeffs[level].shape[0]), pl.ds(1, coeffs[level].shape[1])
-            ],
-            local.at[level],
-        )
-        for level in range(levels)
-    ]
-    own.append(
-        pltpu.make_async_copy(top, tops.at[row_index, col_index], local.at[levels])
-    )
-    for copy in own:
-        copy.start()
-
+    slots = codes.shape[-1]
     for level in range(levels):
         size = patch >> level
         for row in range(size):
             begin = (row << level) * patch * levels + level
-            codes_flat[offsets[level] + row * size : offsets[level] + (row + 1) * size, :] = codes[
-                pl.ds(begin, size, stride=levels << level), :
-            ]
-    codes_flat[offsets[levels] : offsets[levels] + codes_upper.shape[0], :] = codes_upper[...]
+            listed = codes[pl.ds(begin, size, stride=levels << level), :]
+            count = listed_counts[row << level, pl.ds(0, size, stride=1 << level), :]
+            used = lax.broadcasted_iota(jnp.int32, (size, slots), 1) < count[:, level : level + 1]
+            spot = offsets[level] + row * size
+            codes_flat[spot : spot + size, :] = jnp.where(used, listed, -1)
+    begin = 0
+    for step in range(steps):
+        cols = along >> step
+        index = begin + (row_index // 2**step) * cols + col_index // 2**step
+        used = lax.broadcasted_iota(jnp.int32, (1, slots), 1) < counts_upper[index]
+        spot = offsets[levels] + step
+        codes_flat[spot : spot + 1, :] = jnp.where(used, codes_upper[pl.ds(index, 1), :], -1)
+        begin += (across >> step) * cols
     code_lane = lax.broadcasted_iota(jnp.int32, (128, wide), 1) // rank
     code_row = lax.broadcasted_iota(jnp.int32, (128, wide), 0)
     widen = (code_lane == code_row).astype(F32).astype(BF16)
@@ -217,7 +187,41 @@
         top_copy(step, me).start()
         return carry
 
-    lax.fori_loop(1, total, start_top, 0)
+    for number, (sx, sy) in enumerate(SIDES):
+
+        @pl.when(inside(sx, sy))
+        def _():
+            sample_copy(number).start()
+
+    own_basis = twice(basis[...])
+
+    def project(i, carry):
+        rows = samples[i].reshape(patch * vectors, sources)
+        padded[0][i + 2, 1 : 1 + patch // 2] = pair_columns(
+            dot(rows, own_basis, NT), vectors, rank
+        )
+        return carry
+
+    lax.fori_loop(0, patch, project, 0)
+    for level in range(levels):
+        child = padded[level]
+        matrix = twice(transfer[level])
+        cols = patch >> (level + 1)
+        for row in range(cols):
+            grouped = jnp.concatenate(
+                [child[2 * row + 2, 1 : 1 + cols], child[2 * row + 3, 1 : 1 + cols]], axis=-1
+            )
+            lifted = dot(grouped.reshape(-1, 4 * rank), matrix, NT)
+            if level < levels - 1:
+                padded[level + 1][row + 2, 1 : 1 + cols // 2] = pair_columns(
+                    lifted, vectors, rank
+                )
+            else:
+                odd = col_index % 2
+                lane = lax.broadcasted_iota(jnp.int32, lifted.shape, 1)
+                own = (lane >= odd * rank) & (lane < (odd + 1) * rank)
+                tops[row_index, col_index] = jnp.where(own, lifted, 0.0).astype(BF16)
+
     for number, (sx, sy) in enumerate(SIDES):
 
         @pl.when(inside(sx, sy))
@@ -225,11 +229,20 @@
             for level in range(levels):
                 coeff_copy(level, number).start()
 
+    lax.fori_loop(1, total, start_top, 0)
     for number, (sx, sy) in enumerate(SIDES):
-
-        @pl.when(inside(sx, sy))
-        def _():
-            sample_copy(number).start()
+        if sx == 0:
+
+            @pl.when(inside(sx, sy))
+            def _():
+                sample_copy(number, True).start()
+
+    def shift(number, carry):
+        level, part = number // coupling.shape[1], number % coupling.shape[1]
+        shifted[level, part] = coupling[level, part][:, rank:]
+        return carry
+
+    lax.fori_loop(0, coupling.shape[0] * coupling.shape[1], shift, 0)
 
     def near_row(row, row_steps):
         blank = jnp.zeros((1, vectors, sources), BF16)
@@ -254,8 +267,6 @@
 
     lax.fori_loop(1, patch - 1, near_body, 0)
 
-    for copy in own:
-        copy.wait()
     for number, (sx, sy) in enumerate(SIDES):
 
         @pl.when(inside(-sx, -sy))
@@ -305,10 +316,9 @@
     images = []
     begin = offsets[levels]
     for step in range(steps):
-        rows, cols = across >> step, along >> step
         row, col = row_index // 2**step, col_index // 2**step
         slab = window(uppers[step], 2 * (row // 2), col // 2)
-        slab = masked(slab, begin + row * cols + col)
+        slab = masked(slab, begin + step)
         bit = row % 2
         image = []
         for source in (shifted, coupling):
@@ -317,7 +327,6 @@
             )
             image.append(dot(slab, twice(flat), NT))
         images.append(jnp.where(col % 2 == 0, image[0], image[1]))
-        begin += rows * cols
     down = images[-1]
     for step in range(steps - 2, -1, -1):
         row, col = row_index // 2**step, col_index // 2**step
@@ -366,6 +375,8 @@
         @pl.when(inside(-sx, -sy))
         def _():
             sample_copy(number).wait_recv()
+            if sx == 0:
+                sample_copy(number, True).wait_recv()
 
     for rim, column, step in ((left_rim, 0, 0), (right_rim, patch - 1, 2)):
         left = jnp.concatenate(
@@ -397,6 +408,8 @@
             for level in range(levels):
                 coeff_copy(level, number).wait_send()
             sample_copy(number).wait_send()
+            if sx == 0:
+                sample_copy(number, True).wait_send()
 
     def sent_top(step, carry):
         top_copy(step, me).wait_send()
@@ -426,35 +439,19 @@
         steps += 1
     vmem = pl.BlockSpec(memory_space=pltpu.VMEM)
 
-    slot = jnp.arange(codes_local.shape[-1], dtype=jnp.int32)
-    listed = jnp.where(slot < counts_local[..., None], codes_local, -1)
-    listed = listed.reshape(-1, codes_local.shape[-1])
-    listed_upper = jnp.where(slot < counts_upper[..., None], codes_upper, -1)
-
     shapes = [
         jax.ShapeDtypeStruct((patch >> level, patch >> (level + 1), vectors, lanes), BF16)
         for level in range(levels)
     ]
-    shapes.append(jax.ShapeDtypeStruct((vectors, lanes), BF16))
-    coeffs = pl.pallas_call(
-        functools.partial(up_kernel, levels, rank),
-        out_shape=shapes,
-        in_specs=[vmem] * 3,
-        out_specs=[vmem] * len(shapes),
-        compiler_params=pltpu.CompilerParams(vmem_limit_bytes=VMEM_LIMIT),
-        name="up",
-    )(samples, leaf_basis, transfer)
-
     offsets = [0]
     for level in range(levels):
         offsets.append(offsets[-1] + (patch >> level) ** 2)
-    rows = offsets[-1] + codes_upper.shape[0]
+    rows = offsets[-1] + steps
     rows = (rows + 63) // 64 * 64
-    shifted = coupling[..., rank:]
     return pl.pallas_call(
         functools.partial(main_kernel, levels, rank, steps, offsets, (across, along)),
         out_shape=jax.ShapeDtypeStruct(samples.shape, BF16),
-        in_specs=[vmem] * (levels + 10 - 1),
+        in_specs=[vmem] * 4 + [pl.BlockSpec(memory_space=pltpu.SMEM)] + [vmem] * 4,
         out_specs=vmem,
         scratch_shapes=[
             pltpu.VMEM((rows, codes_local.shape[-1]), jnp.int32),
@@ -465,9 +462,9 @@
             pltpu.VMEM((1, patch + 2, vectors, sources), BF16),
             pltpu.VMEM((patch + 2, 1, vectors, sources), BF16),
             pltpu.VMEM((patch + 2, 1, vectors, sources), BF16),
-            pltpu.SemaphoreType.DMA((levels + 1, len(SIDES))),
-            pltpu.SemaphoreType.DMA((levels + 1, len(SIDES))),
-            pltpu.SemaphoreType.DMA((levels + 1,)),
+            pltpu.SemaphoreType.DMA((levels + 2, len(SIDES))),
+            pltpu.SemaphoreType.DMA((levels + 2, len(SIDES))),
+            pltpu.VMEM(coupling.shape[:3] + (6 * rank,), BF16),
             pltpu.SemaphoreType.DMA((across * along,)),
             pltpu.SemaphoreType.DMA((across * along,)),
         ]
@@ -484,7 +481,17 @@
             collective_id=0, has_side_effects=True, vmem_limit_bytes=VMEM_LIMIT
         ),
         name="finish",
-    )(samples, *coeffs, listed, listed_upper, leaf_basis, transfer, coupling, shifted, near_tiles)
+    )(
+        samples,
+        codes_local.reshape(-1, codes_local.shape[-1]),
+        counts_local,
+        codes_upper,
+        counts_upper,
+        leaf_basis,
+        transfer,
+        coupling,
+        near_tiles,
+    )
 
 
 def solution(mesh):

time: 82.1 us -> 72.4 us (0.88)
  Pallas kernels: 69.5 us -> 64.4 us
  other arithmetic: 3.52 us -> 0 us
  local copies, waits for them, and re-layouts: 8.74 us -> 7.77 us
    pallas_call x1 -> x0, Pallas kernels: 7.25 us -> none  [shards(): pl.pallas_call(functools.partial(up_kernel, levels, rank), out_shape=shap...]
    select_n x2 -> x0, other arithmetic: 3.52 us -> none  [the longest x1 2.19 us: shards(): listed = jnp.where(slot < counts_local[..., None], codes_local, -1)]
    pallas_call x1, Pallas kernels: 62.2 us -> 64.4 us  [shards(): pl.pallas_call(functools.partial(main_kernel, levels, rank, steps, offset...]
    slice x1 -> x0, local copies, waits for them, and re-layouts: 2.07 us -> none  [shards(): shifted = coupling[..., rank:]]
    unnamed x5 -> x3, local copies, waits for them, and re-layouts: 6.67 us -> 7.77 us
where the time goes in v3:
time: 72.4 us; the launch traced here: 72.2 us
  Pallas kernels  64.4 us (89%)
  local copies, waits for them, and re-layouts  7.77 us (11%)
    pallas_call x1, Pallas kernels, shards(): pl.pallas_call(functools.partial(main_kernel, levels, rank, steps, offset...  64.4 us
    unnamed x3, local copies, waits for them, and re-layouts  7.77 us

profile of v3, /device:TPU:5, one launch (start us, length us, event | category | flops | bytes accessed | tf_op | source)
XLA Modules:
  0.0 72.2 jit_solution(18441036690185639070)
XLA Ops:
  0.0 1.4 %copy.11.refs_3_ = s32[40,27]{1,0:T(8,128)} copy(s32[40,27]{0,1:T(8,128)} %param.16) | data formatting | bytes 8640 | tf_op args[7]
  1.4 1.6 %copy.10.refs_2_ = s32[16,16,4]{2,1,0:T(8,128)} copy(s32[16,16,4]{1,2,0:T(4,128)} %param.15) | data formatting | bytes 8192 | tf_op args[6]
  3.0 64.4 %finish.1 = bf16[16,16,32,256]{3,2,1,0:T(8,128)(2,1)} custom-call(bf16[16,16,32,256]{3,2,1,0:T(8,128)(2,1)} %refs_0_.1, s32[1024,27]{1,0:T(8,128)} %bitcast.1, s32[16,16,4]{2,1,0:T(8,128)} %copy.10.refs_2_, s32[40,27]{1,0:T(8,128)} %copy.11.refs_3_, s32[40]{0:T(128)} %refs_4_.1, bf16[64,256]{1,0:T(8,128)(2,1)} %refs_5_.1, bf16[5,64,256]{2,1,0:T(8,128)(2,1)} %refs_6_.1, ...), custom_call_target="tpu_custom_call" | custom-call | tf_op jit(solution)/shard_map/finish/pallas_call | solution.py:451
  67.4 4.8 %copy.13 = bf16[16,16,32,256]{3,2,1,0:T(8,128)(2,1)} copy(bf16[16,16,32,256]{3,2,1,0:T(8,128)(2,1)} %finish.1) | data formatting | bytes 8388608

commit v4 on v3

--- a/solution.py
+++ b/solution.py
@@ -52,14 +52,14 @@
 
 def main_kernel(levels, rank, steps, offsets, counts, *refs):
     (samples, codes, listed_counts, codes_upper, counts_upper) = refs[:5]
-    (basis, transfer, coupling, near, out) = refs[5:10]
-    scratch = refs[10:]
+    (basis, transfer, coupling, near, near_out, leaf_down) = refs[5:11]
+    scratch = refs[11:]
     codes_flat, masks, tops, total_near, top_rim, bottom_rim, left_rim, right_rim = scratch[:8]
     send, recv, shifted, top_send, top_recv = scratch[8:13]
     padded = scratch[13 : 13 + levels]
     uppers = scratch[13 + levels : 13 + levels + steps]
-    downs = scratch[13 + levels + steps :]
-    patch, _, vectors, sources = out.shape
+    downs = (leaf_down, *scratch[13 + levels + steps :])
+    patch, _, vectors, sources = samples.shape
     across, along = counts
     total = across * along
     lanes = 2 * rank
@@ -337,38 +337,50 @@
         down = images[step] + part
     spread_top = down.astype(BF16) * low_mask
 
-    def level_row(level, row):
+    def level_rows(level, rows):
         size = patch >> level
         if level == levels - 1:
             parent = spread_top
         else:
-            parent = split_columns(downs[level + 1][row], rank)
+            parent = jnp.concatenate(
+                [split_columns(downs[level + 1][row], rank) for row in rows], axis=0
+            )
         carried = dot(parent, twice(transfer[level]), NN)
-        slabs = [window(padded[level], 2 * row, col) for col in range(size // 2)]
+        slabs = [
+            (row, col, window(padded[level], 2 * row, col))
+            for row in rows
+            for col in range(size // 2)
+        ]
         for row_bit in range(2):
             image = []
             for col_bit in range(2):
-                start = offsets[level] + (2 * row + row_bit) * size + col_bit
                 left = jnp.concatenate(
-                    [masked(slabs[col], start + 2 * col) for col in range(size // 2)], axis=0
+                    [
+                        masked(
+                            slab, offsets[level] + (2 * row + row_bit) * size + col_bit + 2 * col
+                        )
+                        for row, col, slab in slabs
+                    ],
+                    axis=0,
                 )
                 image.append(dot(left, weights(level, row_bit, col_bit), NT))
-            total = jnp.where(low_half(image[0].shape, rank), image[0], image[1])
-            total = total + carried[:, row_bit * lanes : (row_bit + 1) * lanes]
-            downs[level][2 * row + row_bit] = total.astype(BF16).reshape(-1, vectors, lanes)
+            summed = jnp.where(low_half(image[0].shape, rank), image[0], image[1])
+            summed = summed + carried[:, row_bit * lanes : (row_bit + 1) * lanes]
+            summed = summed.astype(BF16).reshape(len(rows), -1, vectors, lanes)
+            for number, row in enumerate(rows):
+                downs[level][2 * row + row_bit] = summed[number]
 
     for level in range(levels - 1, -1, -1):
         count = patch >> (level + 1)
         if count <= 2:
-            for row in range(count):
-                level_row(level, row)
+            level_rows(level, list(range(count)))
         else:
 
-            def body(row, carry, level=level):
-                level_row(level, row)
+            def body(pair, carry, level=level):
+                level_rows(level, [2 * pair, 2 * pair + 1])
                 return carry
 
-            lax.fori_loop(0, count, body, 0)
+            lax.fori_loop(0, count // 2, body, 0)
 
     for number, (sx, sy) in enumerate(SIDES):
 
@@ -392,14 +404,11 @@
         )
         flat = jnp.concatenate([near[step + part] for part in range(3)], axis=-1)
         total_near[row] = total_near[row] + dot(left, flat, NT)
-    basis2 = twice(basis[...])
-
-    def finish(row, carry):
-        summed = total_near[row] + dot(split_columns(downs[0][row], rank), basis2, NN)
-        out[row] = summed.astype(BF16).reshape(patch, vectors, sources)
-        return carry
-
-    lax.fori_loop(0, patch, finish, 0)
+    def round_row(row, carry):
+        near_out[row] = total_near[row].astype(BF16)
+        return carry
+
+    lax.fori_loop(0, patch, round_row, 0)
 
     for number, (sx, sy) in enumerate(SIDES):
 
@@ -416,6 +425,14 @@
         return carry
 
     lax.fori_loop(1, total, sent_top, 0)
+
+
+def finish_kernel(rank, near_sum, leaf_down, basis, out):
+    rows, patch, vectors, sources = out.shape
+    basis2 = twice(basis[...])
+    for row in range(rows):
+        summed = near_sum[row].astype(F32) + dot(split_columns(leaf_down[row], rank), basis2, NN)
+        out[row] = summed.astype(BF16).reshape(patch, vectors, sources)
 
 
 def shards(
@@ -448,11 +465,14 @@
         offsets.append(offsets[-1] + (patch >> level) ** 2)
     rows = offsets[-1] + steps
     rows = (rows + 63) // 64 * 64
-    return pl.pallas_call(
+    near_sum, leaf_down = pl.pallas_call(
         functools.partial(main_kernel, levels, rank, steps, offsets, (across, along)),
-        out_shape=jax.ShapeDtypeStruct(samples.shape, BF16),
+        out_shape=[
+            jax.ShapeDtypeStruct((patch, patch * vectors, sources), BF16),
+            shapes[0],
+        ],
         in_specs=[vmem] * 4 + [pl.BlockSpec(memory_space=pltpu.SMEM)] + [vmem] * 4,
-        out_specs=vmem,
+        out_specs=[vmem, vmem],
         scratch_shapes=[
             pltpu.VMEM((rows, codes_local.shape[-1]), jnp.int32),
             pltpu.VMEM((rows, 36 * rank), F32),
@@ -476,11 +496,11 @@
             pltpu.VMEM(((across >> step) + 4, (along >> (step + 1)) + 2, vectors, lanes), BF16)
             for step in range(steps)
         ]
-        + [pltpu.VMEM(shape.shape, BF16) for shape in shapes[:levels]],
+        + [pltpu.VMEM(shape.shape, BF16) for shape in shapes[1:levels]],
         compiler_params=pltpu.CompilerParams(
             collective_id=0, has_side_effects=True, vmem_limit_bytes=VMEM_LIMIT
         ),
-        name="finish",
+        name="main",
     )(
         samples,
         codes_local.reshape(-1, codes_local.shape[-1]),
@@ -492,6 +512,19 @@
         coupling,
         near_tiles,
     )
+    strip = patch // 4
+    return pl.pallas_call(
+        functools.partial(finish_kernel, rank),
+        out_shape=jax.ShapeDtypeStruct(samples.shape, BF16),
+        grid=(patch // strip,),
+        in_specs=[
+            pl.BlockSpec((strip, patch * vectors, sources), lambda i: (i, 0, 0)),
+            pl.BlockSpec((strip, patch // 2, vectors, lanes), lambda i: (i, 0, 0, 0)),
+            pl.BlockSpec((rank, sources), lambda i: (0, 0)),
+        ],
+        out_specs=pl.BlockSpec((strip, patch, vectors, sources), lambda i: (i, 0, 0, 0)),
+        name="finish",
+    )(near_sum, leaf_down, leaf_basis)
 
 
 def solution(mesh):

time: 72.4 us -> 69.1 us (0.954)
  local copies, waits for them, and re-layouts: 7.77 us -> 2.98 us
  Pallas kernels: 64.4 us -> 65.8 us
    pallas_call x0 -> x1, Pallas kernels: none -> 5.78 us  [shards(): pl.pallas_call(functools.partial(finish_kernel, rank), out_shape=jax.Shap...]
    unnamed x3 -> x2, local copies, waits for them, and re-layouts: 7.77 us -> 2.98 us
    pallas_call x1, Pallas kernels: 64.4 us -> 60 us  [shards(): pl.pallas_call(functools.partial(main_kernel, levels, rank, steps, offset...]
where the time goes in v4:
time: 69.1 us; the launch traced here: 68.8 us
  Pallas kernels  65.8 us (95%)
  local copies, waits for them, and re-layouts  2.98 us (4%)
    pallas_call x1, Pallas kernels, shards(): pl.pallas_call(functools.partial(main_kernel, levels, rank, steps, offset...  60 us
    pallas_call x1, Pallas kernels, shards(): pl.pallas_call(functools.partial(finish_kernel, rank), out_shape=jax.Shap...  5.78 us
    unnamed x2, local copies, waits for them, and re-layouts  2.98 us

profile of v4, /device:TPU:5, one launch (start us, length us, event | category | flops | bytes accessed | tf_op | source)
XLA Modules:
  0.0 68.8 jit_solution(4958990716907201901)
XLA Ops:
  0.0 1.4 %copy.11.refs_3_ = s32[40,27]{1,0:T(8,128)} copy(s32[40,27]{0,1:T(8,128)} %param.16) | data formatting | bytes 8640 | tf_op args[7]
  1.4 1.6 %copy.10.refs_2_ = s32[16,16,4]{2,1,0:T(8,128)} copy(s32[16,16,4]{1,2,0:T(4,128)} %param.15) | data formatting | bytes 8192 | tf_op args[6]
  3.0 60.0 %main.1 = (bf16[16,512,256]{2,1,0:T(8,128)(2,1)}, bf16[16,8,32,128]{3,2,1,0:T(8,128)(2,1)}) custom-call(bf16[16,16,32,256]{3,2,1,0:T(8,128)(2,1)} %refs_0_.1, s32[1024,27]{1,0:T(8,128)} %bitcast.1, s32[16,16,4]{2,1,0:T(8,128)} %copy.10.refs_2_, s32[40,27]{1,0:T(8,128)} %copy.11.refs_3_, s32[40]{0:T(128)} %refs_4_.1, bf16[64,256]{1,0:T(8,128)(2,1)} %basis.1, ...), custom_call_target="tpu_custom_call" | custom-call | tf_op jit(solution)/shard_map/main/pallas_call | solution.py:468
  63.0 5.8 %finish.1 = bf16[16,16,32,256]{3,2,1,0:T(8,128)(2,1)} custom-call(bf16[16,512,256]{2,1,0:T(8,128)(2,1)} %get-tuple-element.7.near_sum, bf16[16,8,32,128]{3,2,1,0:T(8,128)(2,1)} %get-tuple-element.8.leaf_down, bf16[64,256]{1,0:T(8,128)(2,1)} %basis.1), custom_call_target="tpu_custom_call" | custom-call | tf_op jit(solution)/shard_map/finish/pallas_call | solution.py:516

commit v5 on v4

--- a/solution.py
+++ b/solution.py
@@ -222,14 +222,14 @@
                 own = (lane >= odd * rank) & (lane < (odd + 1) * rank)
                 tops[row_index, col_index] = jnp.where(own, lifted, 0.0).astype(BF16)
 
-    for number, (sx, sy) in enumerate(SIDES):
-
-        @pl.when(inside(sx, sy))
-        def _():
-            for level in range(levels):
+    lax.fori_loop(1, total, start_top, 0)
+    for level in range(levels - 1, -1, -1):
+        for number, (sx, sy) in enumerate(SIDES):
+
+            @pl.when(inside(sx, sy))
+            def _():
                 coeff_copy(level, number).start()
 
-    lax.fori_loop(1, total, start_top, 0)
     for number, (sx, sy) in enumerate(SIDES):
         if sx == 0:
 
@@ -266,13 +266,6 @@
         return carry
 
     lax.fori_loop(1, patch - 1, near_body, 0)
-
-    for number, (sx, sy) in enumerate(SIDES):
-
-        @pl.when(inside(-sx, -sy))
-        def _():
-            for level in range(levels):
-                coeff_copy(level, number).wait_recv()
 
     def wait_top(step, carry):
         top_copy(step, (me + total - step) % total).wait_recv()
@@ -371,6 +364,12 @@
                 downs[level][2 * row + row_bit] = summed[number]
 
     for level in range(levels - 1, -1, -1):
+        for number, (sx, sy) in enumerate(SIDES):
+
+            @pl.when(inside(-sx, -sy))
+            def _():
+                coeff_copy(level, number).wait_recv()
+
         count = patch >> (level + 1)
         if count <= 2:
             level_rows(level, list(range(count)))

time: 69.1 us -> 63.4 us (0.918)
  Pallas kernels: 65.8 us -> 60.1 us
    pallas_call x1, Pallas kernels: 60 us -> 54.3 us  [shards(): pl.pallas_call(functools.partial(main_kernel, levels, rank, steps, offset...]
where the time goes in v5:
time: 63.4 us; the launch traced here: 63.1 us
  Pallas kernels  60.1 us (95%)
  local copies, waits for them, and re-layouts  2.98 us (5%)
    pallas_call x1, Pallas kernels, shards(): pl.pallas_call(functools.partial(main_kernel, levels, rank, steps, offset...  54.3 us
    pallas_call x1, Pallas kernels, shards(): pl.pallas_call(functools.partial(finish_kernel, rank), out_shape=jax.Shap...  5.78 us
    unnamed x2, local copies, waits for them, and re-layouts  2.98 us

profile of v5, /device:TPU:5, one launch (start us, length us, event | category | flops | bytes accessed | tf_op | source)
XLA Modules:
  0.0 63.1 jit_solution(3928207018251426211)
XLA Ops:
  0.0 1.4 %copy.11.refs_3_ = s32[40,27]{1,0:T(8,128)} copy(s32[40,27]{0,1:T(8,128)} %param.16) | data formatting | bytes 8640 | tf_op args[7]
  1.4 1.6 %copy.10.refs_2_ = s32[16,16,4]{2,1,0:T(8,128)} copy(s32[16,16,4]{1,2,0:T(4,128)} %param.15) | data formatting | bytes 8192 | tf_op args[6]
  3.0 54.3 %main.1 = (bf16[16,512,256]{2,1,0:T(8,128)(2,1)}, bf16[16,8,32,128]{3,2,1,0:T(8,128)(2,1)}) custom-call(bf16[16,16,32,256]{3,2,1,0:T(8,128)(2,1)} %refs_0_.1, s32[1024,27]{1,0:T(8,128)} %bitcast.1, s32[16,16,4]{2,1,0:T(8,128)} %copy.10.refs_2_, s32[40,27]{1,0:T(8,128)} %copy.11.refs_3_, s32[40]{0:T(128)} %refs_4_.1, bf16[64,256]{1,0:T(8,128)(2,1)} %basis.1, ...), custom_call_target="tpu_custom_call" | custom-call | tf_op jit(solution)/shard_map/main/pallas_call | solution.py:467
  57.3 5.8 %finish.1 = bf16[16,16,32,256]{3,2,1,0:T(8,128)(2,1)} custom-call(bf16[16,512,256]{2,1,0:T(8,128)(2,1)} %get-tuple-element.7.near_sum, bf16[16,8,32,128]{3,2,1,0:T(8,128)(2,1)} %get-tuple-element.8.leaf_down, bf16[64,256]{1,0:T(8,128)(2,1)} %basis.1), custom_call_target="tpu_custom_call" | custom-call | tf_op jit(solution)/shard_map/finish/pallas_call | solution.py:515
